TPU v7x, 32 devices: a whole 2x2x4 slice. The times are simulated.
32 devices in a mesh: sp: 4 (over y, x), fsdp: 8 (over z, core).
Axes of the slice: x: 2, y: 2, z: 4, core: 2. Of those that a mesh axis runs over, the one named last changes fastest.
Arguments:
- layer_input: bfloat16 [8, 1024, 2048], P('fsdp', 'sp'), may hold values from -6 to 6
- positions: int32 [8, 1024], P('fsdp'), may hold values from 0 to 1023, as said below
- cotangent: bfloat16 [8, 1024, 2048], P('fsdp', 'sp'), may hold values from -6 to 6
- w_qkv: bfloat16 [2048, 1536], P('fsdp'), may hold values from -0.125 to 0.125
- w_out: bfloat16 [1024, 2048], P('fsdp'), may hold values from -1 to 1
- w_gate: bfloat16 [2048, 4096], P('fsdp'), may hold values from -0.125 to 0.125
- w_up: bfloat16 [2048, 4096], P('fsdp'), may hold values from -0.125 to 0.125
- w_down: bfloat16 [4096, 2048], P('fsdp'), may hold values from -0.09375 to 0.09375
- gain_attn: bfloat16 [2048], P('fsdp'), may hold values from 0.099609375 to 1.8984375
- gain_ffn: bfloat16 [2048], P('fsdp'), may hold values from 0.099609375 to 1.8984375
- gain_query: bfloat16 [64], replicated, may hold values from 1 to 2
- gain_key: bfloat16 [64], replicated, may hold values from 1 to 2
Outputs:
- out: bfloat16 [8, 1024, 2048], P('fsdp', 'sp')
- grad_input: float32 [8, 1024, 2048], P('fsdp', 'sp')
- grad_qkv: float32 [2048, 1536], P(('sp', 'fsdp'))
- grad_out: float32 [1024, 2048], P(('sp', 'fsdp'))
- grad_gate: float32 [2048, 4096], P(('sp', 'fsdp'))
- grad_up: float32 [2048, 4096], P(('sp', 'fsdp'))
- grad_down: float32 [4096, 2048], P(('sp', 'fsdp'))
- grad_gain_attn: float32 [2048], P(('sp', 'fsdp'))
- grad_gain_ffn: float32 [2048], P(('sp', 'fsdp'))
- grad_gain_query: float32 [64], replicated
- grad_gain_key: float32 [64], replicated
Inputs may be any that keep to these rules, and one draw needn't show every extreme that they name: `positions`: in each sequence the first position is 0, and every later position is either 0 (a new document starts) or the previous position plus 1. The first sequence is a single document.
All inputs are finite; a program needn't handle non-finite values.
Results may differ from a plain program's by a relative error of at most 0.015.
The roundings to bfloat16 on the way count: a program that leaves them out, or rounds other values in their place, can miss the bound.
Values may be sent and summed in bfloat16 or wider, within the bound.
A program may use at most 320 MiB of HBM per device.

v0:
```python
import jax
import jax.numpy as jnp
from jax import lax
from jax.sharding import PartitionSpec as P

QUERY_HEADS = 16
KV_HEADS = 4
HD = 64
EPS = 1e-06
f32 = jnp.float32
bf16 = jnp.bfloat16


def rms_scale(values, gain):
    return values * lax.rsqrt(jnp.mean(values * values, axis=-1, keepdims=True) + EPS) * gain


def rope_tables(position_ids):
    half = HD // 2
    frequency = 10000.0 ** (-2.0 * jnp.arange(half, dtype=f32) / HD)
    angles = position_ids.astype(f32)[:, None, None] * frequency
    return (jnp.cos(angles), jnp.sin(angles))


def rotate(values, cosine, sine):
    half = HD // 2
    front, back = (values[..., :half], values[..., half:])
    return jnp.concatenate([front * cosine - back * sine, back * cosine + front * sine], axis=-1)


def over_rows(a, b):
    return lax.dot_general(a, b, (((0,), (0,)), ((), ())), preferred_element_type=f32)


def times_transposed(a, b):
    return lax.dot_general(a, b, (((1,), (1,)), ((), ())), preferred_element_type=f32)


def masked_scores(q, k, position_ids):
    length = q.shape[0]
    scores = jnp.einsum("qgd,td->gqt", q, k, preferred_element_type=f32) * HD ** (-0.5)
    qi = jnp.arange(length, dtype=jnp.int32)[:, None]
    ki = jnp.arange(length, dtype=jnp.int32)[None, :]
    allowed = (ki <= qi) & (qi - ki <= position_ids[:, None])
    return (jnp.where(allowed, scores, -1e30), allowed)


def attend(q, k, v, position_ids):
    masked, _ = masked_scores(q, k, position_ids)
    largest = jnp.max(masked, axis=-1, keepdims=True)
    exponent = jnp.exp(masked - largest)
    total = jnp.sum(exponent, axis=-1, keepdims=True)
    probs = (exponent / total).astype(bf16)
    mixture = jnp.einsum("gqt,td->qgd", probs, v, preferred_element_type=f32)
    return (mixture.astype(bf16), (largest + jnp.log(total))[..., 0])


def attend_back(q, k, v, position_ids, grad_mixture, log_total):
    masked, allowed = masked_scores(q, k, position_ids)
    probs = jnp.exp(masked - log_total[..., None])
    grad_v = jnp.einsum("gqt,qgd->td", probs.astype(bf16), grad_mixture, preferred_element_type=f32)
    grad_p = jnp.einsum("qgd,td->gqt", grad_mixture, v, preferred_element_type=f32)
    inner = jnp.sum(grad_p * probs, axis=-1, keepdims=True)
    grad_s = jnp.where(allowed, probs * (grad_p - inner), 0.0).astype(bf16)
    scale = HD ** (-0.5)
    grad_q = jnp.einsum("gqt,td->qgd", grad_s, k, preferred_element_type=f32) * scale
    grad_k = jnp.einsum("gqt,qgd->td", grad_s, q, preferred_element_type=f32) * scale
    return (grad_q.astype(bf16), grad_k.astype(bf16), grad_v.astype(bf16))


def swap(value, mask, count):
    return lax.ppermute(value, "sp", [(i, i ^ mask) for i in range(count)])


def gather_chunks(chunk, s, count):
    if count != 4:
        return lax.all_gather(chunk, "sp", axis=0)
    half = chunk.shape[0] // 2
    over_x = swap(chunk, 1, count)
    over_y = swap(chunk, 2, count)
    first = swap(over_x[:half], 2, count)
    second = swap(over_y[half:], 1, count)
    stack = jnp.zeros((count,) + chunk.shape, chunk.dtype)
    for mask, part in ((0, chunk), (1, over_x), (2, over_y)):
        stack = lax.dynamic_update_slice_in_dim(stack, part[None], s ^ mask, 0)
    across = jnp.concatenate([first, second], axis=0)
    return lax.dynamic_update_slice_in_dim(stack, across[None], s ^ 3, 0)


def scatter_sum(partial, s, count):
    rows = partial.shape[0] // count
    if count != 4:
        return lax.psum_scatter(partial.astype(bf16), "sp", scatter_dimension=0, tiled=True).astype(
            f32
        )
    half = rows // 2

    def part(mask):
        return lax.dynamic_slice_in_dim(partial, (s ^ mask) * rows, rows, 0)

    across = part(3).astype(bf16)
    from_y = swap(across[:half], 2, count)
    from_x = swap(across[half:], 1, count)
    to_x, to_y = (part(1), part(2))
    to_x = jnp.concatenate([to_x[:half] + from_y.astype(f32), to_x[half:]], axis=0).astype(bf16)
    to_y = jnp.concatenate([to_y[:half], to_y[half:] + from_x.astype(f32)], axis=0).astype(bf16)
    return part(0) + swap(to_x, 1, count).astype(f32) + swap(to_y, 2, count).astype(f32)


def local(
    x_own,
    positions,
    ct_own,
    w_qkv,
    w_out,
    w_gate,
    w_up,
    w_down,
    gain_attn,
    gain_ffn,
    gain_query,
    gain_key,
):
    S, F = (lax.axis_size("sp"), lax.axis_size("fsdp"))
    s = lax.axis_index("sp")
    _, T, D = x_own.shape
    L = positions.shape[1]
    pos = positions[0]
    copies = max(1, S // KV_HEADS)
    QW = QUERY_HEADS * HD
    KW = KV_HEADS * HD
    heads = QUERY_HEADS // S
    qw = heads * HD
    FF = w_gate.shape[1]
    FFs = FF // S
    rows_d = D // (S * F)
    x_own = x_own[0]
    ct_own = ct_own[0]

    def cut(w, start, size, axis):
        return lax.dynamic_slice_in_dim(w, start, size, axis)

    def regroup(w):
        size = w.shape[0] // S
        perm = [(i * F + j, j * S + i) for i in range(S) for j in range(F)]
        return lax.ppermute(cut(w, s * size, size, 0), ("sp", "fsdp"), perm)

    def gather_z(w):
        return lax.all_gather(w, "fsdp", axis=0, tiled=True)

    gains = jnp.pad(jnp.stack([gain_attn, gain_ffn], axis=1), ((0, 0), (0, 126)))
    kv = s // copies
    attn_part = jnp.concatenate(
        [
            cut(w_qkv, s * qw, qw, 1),
            cut(w_qkv, QW + kv * HD, HD, 1),
            cut(w_qkv, QW + KW + kv * HD, HD, 1),
            gains,
        ],
        axis=1,
    )
    attn_full = gather_z(attn_part)
    hw = qw + 2 * HD
    wqkv_s = attn_full[:, :hw]
    g_attn = attn_full[:, hw].astype(f32)
    g_ffn = attn_full[:, hw + 1].astype(f32)
    wout_s = gather_z(regroup(w_out))
    gu_part = jnp.concatenate([cut(w_gate, s * FFs, FFs, 1), cut(w_up, s * FFs, FFs, 1)], axis=1)
    w_gu = gather_z(gu_part)
    w_dn = gather_z(regroup(w_down))
    x_bf = gather_chunks(x_own, s, S).reshape(L, D)
    x_all = x_bf.astype(f32)
    normed = rms_scale(x_all, g_attn).astype(bf16)
    projected = jnp.dot(normed, wqkv_s, preferred_element_type=f32)
    cosine, sine = rope_tables(pos)

    def prep(raw, gain):
        return rotate(rms_scale(raw, gain), cosine, sine)

    q_rot, q_pull = jax.vjp(prep, projected[:, :qw].reshape(L, heads, HD), gain_query.astype(f32))
    k_rot, k_pull = jax.vjp(
        prep, projected[:, qw : qw + HD].reshape(L, 1, HD), gain_key.astype(f32)
    )
    q = q_rot.astype(bf16)
    k = k_rot.astype(bf16)[:, 0]
    v = projected[:, qw + HD :].astype(bf16)
    mixture, log_total = attend(q, k, v, pos)
    mix_s = mixture.reshape(L, qw)
    mix_all = jnp.swapaxes(gather_chunks(mix_s, s, S), 0, 1).reshape(L, QW)
    wout_full = gather_chunks(wout_s, s, S).reshape(QW, D)
    middle = x_all + jnp.dot(mix_all, wout_full, preferred_element_type=f32)
    ffn_in = rms_scale(middle, g_ffn).astype(bf16)
    gu = jnp.dot(ffn_in, w_gu, preferred_element_type=f32)

    def gated(g, u):
        return jax.nn.silu(g) * u

    hidden_val, hidden_pull = jax.vjp(gated, gu[:, :FFs], gu[:, FFs:])
    hidden = hidden_val.astype(bf16)
    ct_all = gather_chunks(ct_own, s, S).reshape(L, D)
    grad_down = over_rows(hidden, ct_all).astype(bf16)
    grad_down = lax.psum_scatter(grad_down, "fsdp", scatter_dimension=0, tiled=True).astype(f32)
    grad_hidden = times_transposed(ct_all, w_dn)
    d_gate, d_up = hidden_pull(grad_hidden)
    d_gu = jnp.concatenate([d_gate.astype(bf16), d_up.astype(bf16)], axis=1)

    def share_rows(grad):
        width = grad.shape[1]
        grad = grad.astype(bf16).reshape(S, F, rows_d, width)
        grad = jnp.swapaxes(grad, 0, 1).reshape(D, width)
        mine = lax.psum_scatter(grad, "fsdp", scatter_dimension=0, tiled=True)
        mine = mine.reshape(S, rows_d, width)
        return lax.all_to_all(mine, "sp", split_axis=0, concat_axis=0)

    grad_gu = share_rows(over_rows(ffn_in, d_gu))
    grad_gate = jnp.swapaxes(grad_gu[:, :, :FFs], 0, 1).reshape(rows_d, FF).astype(f32)
    grad_up = jnp.swapaxes(grad_gu[:, :, FFs:], 0, 1).reshape(rows_d, FF).astype(f32)
    grad_ffn_in = scatter_sum(times_transposed(d_gu, w_gu), s, S)
    out_sum = scatter_sum(jnp.dot(hidden, w_dn, preferred_element_type=f32), s, S)
    middle_own = cut(middle, s * T, T, 0)
    out = (middle_own + out_sum).astype(bf16)
    _, ffn_pull = jax.vjp(rms_scale, middle_own, g_ffn)
    grad_middle, grad_g_ffn = ffn_pull(grad_ffn_in)
    grad_middle = ct_own.astype(f32) + grad_middle
    d_attn = grad_middle.astype(bf16)
    d_mix_tok = times_transposed(d_attn, wout_full).astype(bf16).reshape(T, S, qw)
    d_mix = lax.all_to_all(jnp.swapaxes(d_mix_tok, 0, 1), "sp", split_axis=0, concat_axis=0)
    d_mix = d_mix.reshape(L, heads, HD)
    d_attn_all = gather_chunks(d_attn, s, S).reshape(L, D)
    grad_out = over_rows(mix_s, d_attn_all).astype(bf16)
    grad_out = lax.psum_scatter(grad_out, "fsdp", scatter_dimension=0, tiled=True).astype(f32)
    dq, dk, dv = attend_back(q, k, v, pos, d_mix, log_total)
    dk, dv = (dk.astype(f32), dv.astype(f32))
    if copies > 1:
        groups = [[i * copies + j for j in range(copies)] for i in range(KV_HEADS)]
        dk, dv = lax.psum((dk, dv), "sp", axis_index_groups=groups)
        first = (s % copies == 0).astype(f32)
        dk, dv = (dk * first, dv * first)
    d_q_raw, grad_g_query = q_pull(dq.astype(f32))
    d_k_raw, grad_g_key = k_pull(dk[:, None])
    d_proj = jnp.concatenate([d_q_raw.reshape(L, qw), d_k_raw[:, 0], dv], axis=1).astype(bf16)
    grad_qkv = share_rows(over_rows(normed, d_proj))
    grad_q = jnp.swapaxes(grad_qkv[:, :, :qw], 0, 1).reshape(rows_d, QW)
    grad_k = jnp.swapaxes(grad_qkv[::copies, :, qw : qw + HD], 0, 1).reshape(rows_d, KW)
    grad_v = jnp.swapaxes(grad_qkv[::copies, :, qw + HD :], 0, 1).reshape(rows_d, KW)
    grad_qkv = jnp.concatenate([grad_q, grad_k, grad_v], axis=1).astype(f32)
    d_proj_own = lax.all_to_all(d_proj.reshape(S, T, hw), "sp", split_axis=0, concat_axis=0)
    wqkv_all = gather_chunks(wqkv_s, s, S)
    grad_normed = jnp.einsum("stc,sdc->td", d_proj_own, wqkv_all, preferred_element_type=f32)
    _, attn_pull = jax.vjp(rms_scale, x_own.astype(f32), g_attn)
    grad_x, grad_g_attn = attn_pull(grad_normed)
    grad_input = grad_middle + grad_x
    tiny = jnp.concatenate([grad_g_attn, grad_g_ffn, grad_g_query, grad_g_key])
    tiny = lax.psum(tiny, ("sp", "fsdp"))
    mine = (s * F + lax.axis_index("fsdp")) * rows_d
    return (
        out[None],
        grad_input[None],
        grad_qkv,
        grad_out,
        grad_gate,
        grad_up,
        grad_down,
        lax.dynamic_slice_in_dim(tiny[:D], mine, rows_d, 0),
        lax.dynamic_slice_in_dim(tiny[D : 2 * D], mine, rows_d, 0),
        tiny[2 * D : 2 * D + HD],
        tiny[2 * D + HD :],
    )


def solution(mesh):
    row = P("fsdp", "sp", None)
    shard = P("fsdp", None)
    grad = P(("sp", "fsdp"), None)
    return jax.shard_map(
        local,
        mesh=mesh,
        in_specs=(
            row,
            shard,
            row,
            shard,
            shard,
            shard,
            shard,
            shard,
            P("fsdp"),
            P("fsdp"),
            P(),
            P(),
        ),
        out_specs=(
            row,
            row,
            grad,
            grad,
            grad,
            grad,
            grad,
            P(("sp", "fsdp")),
            P(("sp", "fsdp")),
            P(),
            P(),
        ),
        check_vma=False,
    )
```

profile of v0, /device:TPU:0, one launch (start us, length us, event | category | flops | bytes accessed | tf_op | source)
XLA Modules:
  0.0 656.7 jit_solution(212468918248744938)
XLA Ops:
  16.5 11.6 %collective-permute-start = (bf16[256,2048]{1,0:T(8,128)(2,1)S(1)}, bf16[256,2048]{1,0:T(8,128)(2,1)}, u32[]{:S(2)}, u32[]{:S(2)}) collective-permute-start(bf16[256,2048]{1,0:T(8,128)(2,1)S(1)} %bitcast.265), channel_id=1, source_target_pairs={{0,8},{8,0},{16,24},{24,16},{1,9},{9,1},{17,25},{25,17},{2,10},{10... | collective-permute-start | bytes 3145736 | tf_op jit(solution)/shard_map/ppermute | solution.py:72
  28.2 3.7 collective-permute-start.1
  34.7 2.6 broadcast.254.clone.1
  38.3 2.5 broadcast.254.clone.2
  44.9 21.8 %collective-permute-done.1 = bf16[256,2048]{1,0:T(8,128)(2,1)} collective-permute-done((bf16[256,2048]{1,0:T(8,128)(2,1)S(1)}, bf16[256,2048]{1,0:T(8,128)(2,1)}, u32[]{:S(2)}, u32[]{:S(2)}) %collective-permute-start.1) | collective-permute-done | bytes 1048608 | tf_op jit(solution)/shard_map/ppermute | solution.py:72
  67.8 16.5 %collective-permute-start.3 = (bf16[128,2048]{1,0:T(8,128)(2,1)S(1)}, bf16[128,2048]{1,0:T(8,128)(2,1)S(1)}, u32[]{:S(2)}, u32[]{:S(2)}) collective-permute-start(bf16[128,2048]{1,0:T(8,128)(2,1)S(1)} %slice.186), channel_id=1, source_target_pairs={{0,8},{8,0},{16,24},{24,16},{1,9},{9,1},{17,25},{25,17},{2,10},{10... | collective-permute-start | bytes 1572872 | tf_op jit(solution)/shard_map/ppermute | solution.py:72
  90.8 2.5 collective-permute-start.20
  93.3 2.4 bitcast_dynamic-update-slice_fusion.12
  95.7 2.4 bitcast_dynamic-update-slice_fusion.7
  98.1 2.3 bitcast_dynamic-update-slice_fusion.11
  100.4 2.3 bitcast_dynamic-update-slice_fusion.6
  105.6 3.1 fusion.8
  108.8 2.7 collective-permute-done.20
  113.6 2.6 broadcast.254.clone
  117.3 16.3 %collective-permute-done.10 = bf16[256,2048]{1,0:T(8,128)(2,1)S(1)} collective-permute-done((bf16[256,2048]{1,0:T(8,128)(2,1)}, bf16[256,2048]{1,0:T(8,128)(2,1)S(1)}, u32[]{:S(2)}, u32[]{:S(2)}) %collective-permute-start.10) | collective-permute-done | bytes 1048608 | tf_op jit(solution)/shard_map/ppermute | solution.py:72
  138.6 3.3 fusion.10
  145.8 7.9 %fusion.108 = (f32[4,1024]{1,0:T(4,128)S(1)}, f32[4,1024,1024]{1,2,0:T(8,128)}) fusion(bf16[1024,4,32]{0,2,1:T(8,128)(2,1)S(1)} %get-tuple-element.39, bf16[1024,4,32]{0,2,1:T(8,128)(2,1)S(1)} %get-tuple-element.38, bf16[1024,32]{0,1:T(8,128)(2,1)S(1)} %get-tuple-element.51, bf16[1024,32]{0,1:T(8,128)(2,1)S(1)} %get-tuple-element.50, ...), kind=kOutput, calls=%fused_computation.228 | convolution fusion | flops 550760448 | bytes 18497536 | tf_op jit(solution)/shard_map/qgd,td->gqt/dot_general | solution.py:41
  153.7 8.1 %fusion.4 = f32[4,1024]{1,0:T(4,128)S(1)} fusion(f32[4,1024,1024]{1,2,0:T(8,128)} %get-tuple-element.61, f32[4,1024]{1,0:T(4,128)S(1)} %get-tuple-element.60), kind=kLoop, calls=%fused_computation.10 | loop fusion | flops 8384512 | bytes 16809984 | tf_op jit(solution)/shard_map/reduce_sum | solution.py:52
  161.8 7.5 %fusion.35 = bf16[64,4,1024]{2,0,1:T(8,128)(2,1)S(1)} fusion(f32[4,1024,1024]{1,2,0:T(8,128)} %get-tuple-element.61, f32[4,1024]{1,0:T(4,128)S(1)} %fusion.4, f32[4,1024]{1,0:T(4,128)S(1)} %get-tuple-element.60, f32[1024,384]{0,1:T(8,128)S(1)} %fusion.100), kind=kOutput, calls=%fused_computation.76 | convolution fusion | flops 549715968 | bytes 17465344 | tf_op jit(solution)/shard_map/gqt,td->qgd/dot_general | solution.py:54
  170.4 2.2 collective-permute-start.4
  175.3 2.3 fusion.54
  178.1 8.0 %collective-permute-done.5 = bf16[1024,256]{1,0:T(8,128)(2,1)} collective-permute-done((bf16[1024,256]{1,0:T(8,128)(2,1)}, bf16[1024,256]{1,0:T(8,128)(2,1)}, u32[]{:S(2)}, u32[]{:S(2)}) %collective-permute-start.5) | collective-permute-done | bytes 524320 | tf_op jit(solution)/shard_map/ppermute | solution.py:72
  195.2 9.9 %multiply_reduce_fusion = (f32[1024]{0:T(1024)S(1)}, f32[1024,2048]{1,0:T(8,128)}) fusion(bf16[4,256,2048]{2,1,0:T(8,128)(2,1)} %fusion.54, bf16[4,1024,256]{2,1,0:T(8,128)(2,1)S(1)} %fusion.62, bf16[4,256,2048]{2,1,0:T(8,128)(2,1)} %fusion.53), kind=kOutput, calls=%fused_computation.22 | convolution fusion | flops 4303354880 | bytes 18878464 | tf_op jit(solution)/shard_map/dot_general | solution.py:191
  205.1 16.0 %fusion.102 = f32[1024,2048]{1,0:T(8,128)} fusion(bf16[2048,2048]{1,0:T(8,128)(2,1)} %all-gather.9.cloned.1.call-done, f32[1024,2048]{1,0:T(8,128)} %get-tuple-element.63, f32[2048]{0:T(1024)S(1)} %get-tuple-element.15, f32[1024]{0:T(1024)S(1)} %add_rsqrt_fusion), kind=kOutput, calls=%fused_computation.223 | convolution fusion | flops 8596226048 | bytes 25178112 | tf_op jit(solution)/shard_map/dot_general | solution.py:193
  221.2 14.7 %fusion.18 = (bf16[1024,1024]{1,0:T(8,128)(2,1)}, bf16[1024,1024]{1,0:T(8,128)(2,1)}, bf16[1024,1024]{1,0:T(8,128)(2,1)}) fusion(f32[1024,2048]{1,0:T(8,128)} %fusion.102, bf16[1024,2048]{1,0:T(8,128)(2,1)} %bitcast.31, bf16[1024,2048]{1,0:T(8,128)(2,1)} %all-gather.11.cloned.1.call-done), kind=kOutput, calls=%fused_computation.30 | convolution fusion | flops 4311744512 | bytes 23068672 | tf_op jit(solution)/shard_map/dot_general | solution.py:36
  235.9 10.9 %fusion.21 = f32[1024,2048]{1,0:T(8,128)S(1)} fusion(bf16[2048,2048]{1,0:T(8,128)(2,1)S(1)} %copy-done.50, bf16[1024,1024]{1,0:T(8,128)(2,1)} %get-tuple-element.25, bf16[1024,1024]{1,0:T(8,128)(2,1)} %get-tuple-element.24), kind=kOutput, calls=%fused_computation.48 | convolution fusion | flops 8598323200 | bytes 20971520 | tf_op jit(solution)/shard_map/dot_general | solution.py:36
  252.0 6.1 fusion.109
  265.6 7.7 %collective-permute-done.14 = bf16[128,2048]{1,0:T(8,128)(2,1)S(1)} collective-permute-done((bf16[128,2048]{1,0:T(8,128)(2,1)S(1)}, bf16[128,2048]{1,0:T(8,128)(2,1)S(1)}, u32[]{:S(2)}, u32[]{:S(2)}) %collective-permute-start.14) | collective-permute-done | bytes 524320 | tf_op jit(solution)/shard_map/ppermute | solution.py:72
  280.9 14.9 %collective-permute-done.25 = bf16[256,2048]{1,0:T(8,128)(2,1)S(1)} collective-permute-done((bf16[256,2048]{1,0:T(8,128)(2,1)}, bf16[256,2048]{1,0:T(8,128)(2,1)S(1)}, u32[]{:S(2)}, u32[]{:S(2)}) %collective-permute-start.25) | collective-permute-done | bytes 1048608 | tf_op jit(solution)/shard_map/ppermute | solution.py:72
  297.6 17.4 %collective-permute-done.17 = bf16[256,2048]{1,0:T(8,128)(2,1)} collective-permute-done((bf16[256,2048]{1,0:T(8,128)(2,1)}, bf16[256,2048]{1,0:T(8,128)(2,1)}, u32[]{:S(2)}, u32[]{:S(2)}) %collective-permute-start.17) | collective-permute-done | bytes 1048608 | tf_op jit(solution)/shard_map/ppermute | solution.py:72
  316.4 6.6 %multiply_reduce_fusion.1 = (f32[2048]{0:T(1024)}, f32[256]{0:T(256)S(1)}, bf16[1,256,2048]{2,1,0:T(8,128)(2,1)}) fusion(f32[1024,2048]{1,0:T(8,128)} %get-tuple-element.63, s32[]{:T(128)S(6)} %select_n.92, f32[256]{0:T(256)S(1)} %fusion.90, bf16[256,2048]{1,0:T(8,128)(2,1)S(1)} %collective-permute-done.25, bf16[256,2048]{1,0:T(8,128)(2,1)} %collective-permute-done.23, ...), kind=kLoop, calls=%fused_computation.58 | loop fusion | flops 8386304 | bytes 11552772 | tf_op jit(solution)/shard_map/transpose(jvp())/reduce_sum | solution.py:15
  324.2 5.3 bitcast_dynamic-update-slice_fusion.5
  329.5 5.3 convolution_convert_fusion.4
  335.7 3.5 all-to-all-start
  339.7 6.0 all-to-all-done
  348.1 8.1 %fusion.85 = f32[1024,1024,4]{1,0,2:T(8,128)} fusion(bf16[1024,4,64]{0,2,1:T(8,128)(2,1)S(1)} %reshape.378, f32[1024,384]{0,1:T(8,128)S(1)} %fusion.100), kind=kOutput, calls=%fused_computation.185 | convolution fusion | flops 536870912 | bytes 17432576 | tf_op jit(solution)/shard_map/qgd,td->gqt/dot_general | solution.py:62
  356.3 8.4 %fusion.42 = bf16[1024,64]{0,1:T(8,128)(2,1)S(1)} fusion(bf16[1024,4,64]{0,2,1:T(8,128)(2,1)S(1)} %reshape.378, f32[4,1024,1024]{1,2,0:T(8,128)} %get-tuple-element.61, f32[4,1024]{1,0:T(4,128)S(1)} %log_add_fusion), kind=kOutput, calls=%fused_computation.81 | convolution fusion | flops 545325056 | bytes 17448960 | tf_op jit(solution)/shard_map/gqt,qgd->td/dot_general | solution.py:61
  364.7 23.8 %fusion.46 = f32[1024,1,64]{0,2,1:T(8,128)S(1)} fusion(f32[1024,1024,4]{1,0,2:T(8,128)} %fusion.85, f32[4,1024,1024]{1,2,0:T(8,128)} %get-tuple-element.61, f32[4,1024]{1,0:T(4,128)S(1)} %log_add_fusion, pred[1024,1024]{0,1:T(8,128)(4,1)} %fusion.20, bf16[1024,4,32]{0,2,1:T(8,128)(2,1)} %copy-done.25, bf16[1024,4,32]{0,2,1:T(8,128)(2,1)S(1)} %get-tuple-element.38), kind=kOutput, calls=%fused_computation.83 | convolution fusion | flops 567481344 | bytes 35405824 | tf_op jit(solution)/shard_map/gqt,qgd->td/dot_general | solution.py:67
  388.6 27.0 %fusion.34 = f32[1024,4,64]{0,2,1:T(8,128)} fusion(f32[1024,1024,4]{1,0,2:T(8,128)} %fusion.85, f32[4,1024,1024]{1,2,0:T(8,128)} %get-tuple-element.61, f32[4,1024]{1,0:T(4,128)} %copy-done.26, pred[1024,1024]{0,1:T(8,128)(4,1)} %fusion.20, bf16[1024,32]{0,1:T(8,128)(2,1)S(1)} %copy-done.39, bf16[1024,32]{0,1:T(8,128)(2,1)S(1)} %copy-done.37), kind=kOutput, calls=%fused_computation.74 | convolution fusion | flops 567284736 | bytes 35799040 | tf_op jit(solution)/shard_map/gqt,td->qgd/dot_general | solution.py:66
  423.0 2.5 convolution_convert_fusion.2
  426.9 15.1 %convolution_convert_fusion = bf16[2048,2048]{1,0:T(8,128)(2,1)} fusion(bf16[1024,1024]{1,0:T(8,128)(2,1)} %get-tuple-element.25, bf16[1024,1024]{1,0:T(8,128)(2,1)} %get-tuple-element.24, f32[1024,2048]{1,0:T(8,128)} %get-tuple-element.63, f32[2048]{0:T(1024)S(1)} %copy-done.33, f32[1024]{0:T(1024)S(1)} %copy-done.48), kind=kOutput, calls=%fused_computation.26 | convolution fusion | flops 8608808960 | bytes 20983808 | tf_op jit(solution)/shard_map/dot_general | solution.py:32
  442.0 8.4 %copy.92 = bf16[4,8,64,2048]{3,2,0,1:T(8,128)(2,1)} copy(bf16[4,8,64,2048]{3,2,1,0:T(8,128)(2,1)} %bitcast.267) | data formatting | bytes 16777216 | tf_op jit(solution)/shard_map/reshape | solution.py:209
  452.6 20.1 %collective-permute-done.31 = bf16[256,2048]{1,0:T(8,128)(2,1)S(1)} collective-permute-done((bf16[256,2048]{1,0:T(8,128)(2,1)}, bf16[256,2048]{1,0:T(8,128)(2,1)S(1)}, u32[]{:S(2)}, u32[]{:S(2)}) %collective-permute-start.31) | collective-permute-done | bytes 1048608 | tf_op jit(solution)/shard_map/ppermute | solution.py:72
  472.8 2.3 collective-permute-start.33
  478.6 5.2 collective-permute-done.33
  486.7 4.6 convolution_convert_fusion.3
  491.3 8.6 %convolution_convert_fusion.1 = bf16[1024,2048]{1,0:T(8,128)(2,1)} fusion(bf16[1024,1024]{1,0:T(8,128)(2,1)S(1)} %copy-done.54, bf16[1024,2048]{1,0:T(8,128)(2,1)} %bitcast.31), kind=kOutput, calls=%fused_computation.39 | convolution fusion | flops 4297064448 | bytes 10485760 | tf_op jit(solution)/shard_map/dot_general | solution.py:32
  499.9 2.8 slice.188
  505.2 3.2 broadcast_in_dim.152
  508.5 2.8 bitcast_dynamic-update-slice_fusion.2
  511.3 22.3 %collective-permute-done.27 = bf16[2048,384]{1,0:T(8,128)(2,1)} collective-permute-done((bf16[2048,384]{1,0:T(8,128)(2,1)}, bf16[2048,384]{1,0:T(8,128)(2,1)}, u32[]{:S(2)}, u32[]{:S(2)}) %collective-permute-start.27) | collective-permute-done | bytes 1572896 | tf_op jit(solution)/shard_map/ppermute | solution.py:72
  537.9 2.4 collective-permute-start.28
  540.3 2.7 bitcast_dynamic-update-slice_fusion.1
  545.2 3.6 all-to-all-start.1
  548.8 2.7 bitcast_dynamic-update-slice_fusion
  551.6 3.1 collective-permute-done.29
  556.1 2.7 fusion.30
  559.2 6.0 fusion.28
  565.3 52.6 %psum.7 = f32[4224]{0:T(1024)S(1)} all-reduce(f32[4224]{0:T(1024)S(1)} %concatenate.101), channel_id=1, replica_groups=mesh['sp'=4,'fsdp'=8] {'sp','fsdp'}, use_global_device_ids=true, to_apply=%region_21.22 | all-reduce | flops 4224 | bytes 33792 | tf_op jit(solution)/shard_map/psum | solution.py:254
  617.9 4.1 fusion.24
  622.1 4.4 all-to-all-start.2
  626.5 5.2 all-to-all-done.2
  631.7 3.5 all-to-all-start.3
  643.4 3.9 all-to-all-done.3
  (300 shorter events, 120.1 us)
Async XLA Ops:
  7.2 24.9 %copy-start = (bf16[512,2048]{1,0:T(8,128)(2,1)S(1)}, bf16[512,2048]{1,0:T(8,128)(2,1)}, u32[]{:S(2)}) copy-start(bf16[512,2048]{1,0:T(8,128)(2,1)} %param.19) | copy-start | bytes 6291460
  7.2 27.4 %copy-start.52 = (bf16[64]{0:T(256)(128)(2,1)S(1)}, bf16[64]{0:T(256)(128)(2,1)}, u32[]{:S(2)}) copy-start(bf16[64]{0:T(256)(128)(2,1)} %param.22) | copy-start | bytes 388
  7.2 27.4 %copy-start.42 = (s32[1,1024]{1,0:T(1,128)S(1)}, s32[1,1024]{1,0:T(1,128)}, u32[]{:S(2)}) copy-start(s32[1,1024]{1,0:T(1,128)} %param.13) | copy-start | bytes 12292
  7.2 27.4 %copy-start.53 = (bf16[64]{0:T(256)(128)(2,1)S(1)}, bf16[64]{0:T(256)(128)(2,1)}, u32[]{:S(2)}) copy-start(bf16[64]{0:T(256)(128)(2,1)} %param.23) | copy-start | bytes 388
  7.2 96.6 %all-gather.7.cloned.1.call-start = ((), (), s32[]{:S(2)}) async-start(), calls=%async_computation.9 | async-start | bytes 1179648 | tf_op jit(solution)/shard_map/all_gather | solution.py:149
  8.4 0.7 collective-permute-start.8
  9.8 126.9 %all-gather.5.cloned.1.call-start = ((), (), s32[]{:S(2)}) async-start(), calls=%async_computation.8 | async-start | bytes 2359296 | tf_op jit(solution)/shard_map/all_gather | solution.py:149
  14.1 191.0 %all-gather.9.cloned.1.call-start = ((), (), s32[]{:S(2)}) async-start(), calls=%async_computation.10 | async-start | bytes 9437184 | tf_op jit(solution)/shard_map/all_gather | solution.py:149
  16.5 204.7 %all-gather.11.cloned.1.call-start = ((), (), s32[]{:S(2)}) async-start(), calls=%async_computation.11 | async-start | bytes 4718592 | tf_op jit(solution)/shard_map/all_gather | solution.py:149
  16.5 67.8 %collective-permute-start = (bf16[256,2048]{1,0:T(8,128)(2,1)S(1)}, bf16[256,2048]{1,0:T(8,128)(2,1)}, u32[]{:S(2)}, u32[]{:S(2)}) collective-permute-start(bf16[256,2048]{1,0:T(8,128)(2,1)S(1)} %bitcast.265), channel_id=1, source_target_pairs={{0,8},{8,0},{16,24},{24,16},{1,9},{9,1},{17,25},{25,17},{2,10},{10... | collective-permute-start | bytes 3145736 | tf_op jit(solution)/shard_map/ppermute | solution.py:72
  28.2 38.6 %collective-permute-start.1 = (bf16[256,2048]{1,0:T(8,128)(2,1)S(1)}, bf16[256,2048]{1,0:T(8,128)(2,1)}, u32[]{:S(2)}, u32[]{:S(2)}) collective-permute-start(bf16[256,2048]{1,0:T(8,128)(2,1)S(1)} %bitcast.266), channel_id=1, source_target_pairs={{0,16},{8,24},{16,0},{24,8},{1,17},{9,25},{17,1},{25,9},{2,18},{10... | collective-permute-start | bytes 3145736 | tf_op jit(solution)/shard_map/ppermute | solution.py:72
  31.9 57.0 %collective-permute-start.18 = (bf16[256,2048]{1,0:T(8,128)(2,1)}, bf16[256,2048]{1,0:T(8,128)(2,1)}, u32[]{:S(2)}, u32[]{:S(2)}) collective-permute-start(bf16[256,2048]{1,0:T(8,128)(2,1)} %bitcast.269), channel_id=1, source_target_pairs={{0,8},{8,0},{16,24},{24,16},{1,9},{9,1},{17,25},{25,17},{2,10},{10... | collective-permute-start | bytes 3145736 | tf_op jit(solution)/shard_map/ppermute | solution.py:72
  32.0 54.7 %collective-permute-start.19 = (bf16[256,2048]{1,0:T(8,128)(2,1)}, bf16[256,2048]{1,0:T(8,128)(2,1)}, u32[]{:S(2)}, u32[]{:S(2)}) collective-permute-start(bf16[256,2048]{1,0:T(8,128)(2,1)} %bitcast.270), channel_id=1, source_target_pairs={{0,16},{8,24},{16,0},{24,8},{1,17},{9,25},{17,1},{25,9},{2,18},{10... | collective-permute-start | bytes 3145736 | tf_op jit(solution)/shard_map/ppermute | solution.py:72
  32.9 11.2 %collective-permute-start.13 = (bf16[128,2048]{1,0:T(8,128)(2,1)}, bf16[128,2048]{1,0:T(8,128)(2,1)S(1)}, u32[]{:S(2)}, u32[]{:S(2)}) collective-permute-start(bf16[128,2048]{1,0:T(8,128)(2,1)} %constant_dynamic-slice_fusion), channel_id=1, source_target_pairs={{0,0},{1,4},{2,8},{3,12},{4,16},{5,20},{6,24},{7,28},{8,1},{9,5},{... | collective-permute-start | bytes 1572872 | tf_op jit(solution)/shard_map/ppermute | solution.py:146
  34.6 110.7 %copy-start.43 = (f32[64]{0:T(128)}, f32[64]{0:T(128)S(1)}, u32[]{:S(2)}) copy-start(f32[64]{0:T(128)S(1)} %convert_element_type.196) | copy-start | bytes 772
  34.6 110.1 %copy-start.34 = (f32[1024]{0:T(1024)}, f32[1024]{0:T(1024)S(1)}, u32[]{:S(2)}) copy-start(f32[1024]{0:T(1024)S(1)} %convert_element_type.195) | copy-start | bytes 12292
  34.6 110.0 %copy-start.46 = (f32[64]{0:T(128)}, f32[64]{0:T(128)S(1)}, u32[]{:S(2)}) copy-start(f32[64]{0:T(128)S(1)} %convert_element_type.194) | copy-start | bytes 772
  34.7 110.1 %copy-start.45 = (f32[32]{0:T(128)}, f32[32]{0:T(128)S(1)}, u32[]{:S(2)}) copy-start(f32[32]{0:T(128)S(1)} %multiply_power_fusion) | copy-start | bytes 388
  42.4 103.2 %copy-start.14 = (f32[1024,32]{0,1:T(8,128)}, f32[1024,32]{0,1:T(8,128)S(1)}, u32[]{:S(2)}) copy-start(f32[1024,32]{0,1:T(8,128)S(1)} %get-tuple-element.58) | copy-start | bytes 393220
  42.5 103.2 %copy-start.16 = (f32[1024,32]{0,1:T(8,128)}, f32[1024,32]{0,1:T(8,128)S(1)}, u32[]{:S(2)}) copy-start(f32[1024,32]{0,1:T(8,128)S(1)} %get-tuple-element.59) | copy-start | bytes 393220
  67.8 34.9 %collective-permute-start.3 = (bf16[128,2048]{1,0:T(8,128)(2,1)S(1)}, bf16[128,2048]{1,0:T(8,128)(2,1)S(1)}, u32[]{:S(2)}, u32[]{:S(2)}) collective-permute-start(bf16[128,2048]{1,0:T(8,128)(2,1)S(1)} %slice.186), channel_id=1, source_target_pairs={{0,8},{8,0},{16,24},{24,16},{1,9},{9,1},{17,25},{25,17},{2,10},{10... | collective-permute-start | bytes 1572872 | tf_op jit(solution)/shard_map/ppermute | solution.py:72
  85.4 17.4 %collective-permute-start.2 = (bf16[128,2048]{1,0:T(8,128)(2,1)S(1)}, bf16[128,2048]{1,0:T(8,128)(2,1)S(1)}, u32[]{:S(2)}, u32[]{:S(2)}) collective-permute-start(bf16[128,2048]{1,0:T(8,128)(2,1)S(1)} %slice.185), channel_id=1, source_target_pairs={{0,16},{8,24},{16,0},{24,8},{1,17},{9,25},{17,1},{25,9},{2,18},{10... | collective-permute-start | bytes 1572872 | tf_op jit(solution)/shard_map/ppermute | solution.py:72
  88.6 20.2 %collective-permute-start.21 = (bf16[128,2048]{1,0:T(8,128)(2,1)}, bf16[128,2048]{1,0:T(8,128)(2,1)S(1)}, u32[]{:S(2)}, u32[]{:S(2)}) collective-permute-start(bf16[128,2048]{1,0:T(8,128)(2,1)} %slice.206), channel_id=1, source_target_pairs={{0,8},{8,0},{16,24},{24,16},{1,9},{9,1},{17,25},{25,17},{2,10},{10... | collective-permute-start | bytes 1572872 | tf_op jit(solution)/shard_map/ppermute | solution.py:72
  90.8 20.7 %collective-permute-start.20 = (bf16[128,2048]{1,0:T(8,128)(2,1)}, bf16[128,2048]{1,0:T(8,128)(2,1)}, u32[]{:S(2)}, u32[]{:S(2)}) collective-permute-start(bf16[128,2048]{1,0:T(8,128)(2,1)} %slice.205), channel_id=1, source_target_pairs={{0,16},{8,24},{16,0},{24,8},{1,17},{9,25},{17,1},{25,9},{2,18},{10... | collective-permute-start | bytes 1572872 | tf_op jit(solution)/shard_map/ppermute | solution.py:72
  103.9 30.5 %collective-permute-start.9 = (bf16[256,2048]{1,0:T(8,128)(2,1)}, bf16[256,2048]{1,0:T(8,128)(2,1)S(1)}, u32[]{:S(2)}, u32[]{:S(2)}) collective-permute-start(bf16[256,2048]{1,0:T(8,128)(2,1)} %all-gather.7.cloned.1.call-done), channel_id=1, source_target_pairs={{0,8},{8,0},{16,24},{24,16},{1,9},{9,1},{17,25},{25,17},{2,10},{10... | collective-permute-start | bytes 3145736 | tf_op jit(solution)/shard_map/ppermute | solution.py:72
  105.5 28.0 %collective-permute-start.10 = (bf16[256,2048]{1,0:T(8,128)(2,1)}, bf16[256,2048]{1,0:T(8,128)(2,1)S(1)}, u32[]{:S(2)}, u32[]{:S(2)}) collective-permute-start(bf16[256,2048]{1,0:T(8,128)(2,1)} %all-gather.7.cloned.1.call-done), channel_id=1, source_target_pairs={{0,16},{8,24},{16,0},{24,8},{1,17},{9,25},{17,1},{25,9},{2,18},{10... | collective-permute-start | bytes 3145736 | tf_op jit(solution)/shard_map/ppermute | solution.py:72
  134.4 40.9 %collective-permute-start.12 = (bf16[128,2048]{1,0:T(8,128)(2,1)}, bf16[128,2048]{1,0:T(8,128)(2,1)}, u32[]{:S(2)}, u32[]{:S(2)}) collective-permute-start(bf16[128,2048]{1,0:T(8,128)(2,1)} %slice.199), channel_id=1, source_target_pairs={{0,8},{8,0},{16,24},{24,16},{1,9},{9,1},{17,25},{25,17},{2,10},{10... | collective-permute-start | bytes 1572872 | tf_op jit(solution)/shard_map/ppermute | solution.py:72
  135.2 40.1 %collective-permute-start.11 = (bf16[128,2048]{1,0:T(8,128)(2,1)}, bf16[128,2048]{1,0:T(8,128)(2,1)}, u32[]{:S(2)}, u32[]{:S(2)}) collective-permute-start(bf16[128,2048]{1,0:T(8,128)(2,1)} %slice.198), channel_id=1, source_target_pairs={{0,16},{8,24},{16,0},{24,8},{1,17},{9,25},{17,1},{25,9},{2,18},{10... | collective-permute-start | bytes 1572872 | tf_op jit(solution)/shard_map/ppermute | solution.py:72
  138.6 185.0 %copy-start.32 = (f32[2048]{0:T(1024)}, f32[2048]{0:T(1024)S(1)}, u32[]{:S(2)}) copy-start(f32[2048]{0:T(1024)S(1)} %get-tuple-element.15) | copy-start | bytes 24580
  170.4 17.0 %collective-permute-start.4 = (bf16[1024,256]{1,0:T(8,128)(2,1)}, bf16[1024,256]{1,0:T(8,128)(2,1)}, u32[]{:S(2)}, u32[]{:S(2)}) collective-permute-start(bf16[1024,256]{1,0:T(8,128)(2,1)} %copy.76), channel_id=1, source_target_pairs={{0,8},{8,0},{16,24},{24,16},{1,9},{9,1},{17,25},{25,17},{2,10},{10... | collective-permute-start | bytes 1572872 | tf_op jit(solution)/shard_map/ppermute | solution.py:72
  172.5 13.5 %collective-permute-start.5 = (bf16[1024,256]{1,0:T(8,128)(2,1)}, bf16[1024,256]{1,0:T(8,128)(2,1)}, u32[]{:S(2)}, u32[]{:S(2)}) collective-permute-start(bf16[1024,256]{1,0:T(8,128)(2,1)} %copy.76), channel_id=1, source_target_pairs={{0,16},{8,24},{16,0},{24,8},{1,17},{9,25},{17,1},{25,9},{2,18},{10... | collective-permute-start | bytes 1572872 | tf_op jit(solution)/shard_map/ppermute | solution.py:72
  187.0 6.7 %collective-permute-start.7 = (bf16[512,256]{1,0:T(8,128)(2,1)S(1)}, bf16[512,256]{1,0:T(8,128)(2,1)S(1)}, u32[]{:S(2)}, u32[]{:S(2)}) collective-permute-start(bf16[512,256]{1,0:T(8,128)(2,1)S(1)} %slice.197), channel_id=1, source_target_pairs={{0,8},{8,0},{16,24},{24,16},{1,9},{9,1},{17,25},{25,17},{2,10},{10... | collective-permute-start | bytes 786440 | tf_op jit(solution)/shard_map/ppermute | solution.py:72
  188.4 6.8 %collective-permute-start.6 = (bf16[512,256]{1,0:T(8,128)(2,1)S(1)}, bf16[512,256]{1,0:T(8,128)(2,1)S(1)}, u32[]{:S(2)}, u32[]{:S(2)}) collective-permute-start(bf16[512,256]{1,0:T(8,128)(2,1)S(1)} %slice.196), channel_id=1, source_target_pairs={{0,16},{8,24},{16,0},{24,8},{1,17},{9,25},{17,1},{25,9},{2,18},{10... | collective-permute-start | bytes 786440 | tf_op jit(solution)/shard_map/ppermute | solution.py:72
  247.0 14.4 %collective-permute-start.22 = (bf16[128,2048]{1,0:T(8,128)(2,1)S(1)}, bf16[128,2048]{1,0:T(8,128)(2,1)S(1)}, u32[]{:S(2)}, u32[]{:S(2)}) collective-permute-start(bf16[128,2048]{1,0:T(8,128)(2,1)S(1)} %get-tuple-element.42), channel_id=1, source_target_pairs={{0,16},{8,24},{16,0},{24,8},{1,17},{9,25},{17,1},{25,9},{2,18},{10... | collective-permute-start | bytes 1572872 | tf_op jit(solution)/shard_map/ppermute | solution.py:72
  248.8 12.7 %collective-permute-start.24 = (bf16[128,2048]{1,0:T(8,128)(2,1)S(1)}, bf16[128,2048]{1,0:T(8,128)(2,1)S(1)}, u32[]{:S(2)}, u32[]{:S(2)}) collective-permute-start(bf16[128,2048]{1,0:T(8,128)(2,1)S(1)} %get-tuple-element.43), channel_id=1, source_target_pairs={{0,8},{8,0},{16,24},{24,16},{1,9},{9,1},{17,25},{25,17},{2,10},{10... | collective-permute-start | bytes 1572872 | tf_op jit(solution)/shard_map/ppermute | solution.py:72
  258.4 14.9 %collective-permute-start.14 = (bf16[128,2048]{1,0:T(8,128)(2,1)S(1)}, bf16[128,2048]{1,0:T(8,128)(2,1)S(1)}, u32[]{:S(2)}, u32[]{:S(2)}) collective-permute-start(bf16[128,2048]{1,0:T(8,128)(2,1)S(1)} %get-tuple-element.44), channel_id=1, source_target_pairs={{0,16},{8,24},{16,0},{24,8},{1,17},{9,25},{17,1},{25,9},{2,18},{10... | collective-permute-start | bytes 1572872 | tf_op jit(solution)/shard_map/ppermute | solution.py:72
  260.1 14.9 %collective-permute-start.16 = (bf16[128,2048]{1,0:T(8,128)(2,1)S(1)}, bf16[128,2048]{1,0:T(8,128)(2,1)S(1)}, u32[]{:S(2)}, u32[]{:S(2)}) collective-permute-start(bf16[128,2048]{1,0:T(8,128)(2,1)S(1)} %get-tuple-element.45), channel_id=1, source_target_pairs={{0,8},{8,0},{16,24},{24,16},{1,9},{9,1},{17,25},{25,17},{2,10},{10... | collective-permute-start | bytes 1572872 | tf_op jit(solution)/shard_map/ppermute | solution.py:72
  262.9 32.9 %collective-permute-start.25 = (bf16[256,2048]{1,0:T(8,128)(2,1)}, bf16[256,2048]{1,0:T(8,128)(2,1)S(1)}, u32[]{:S(2)}, u32[]{:S(2)}) collective-permute-start(bf16[256,2048]{1,0:T(8,128)(2,1)} %pad_maximum_fusion.7), channel_id=1, source_target_pairs={{0,16},{8,24},{16,0},{24,8},{1,17},{9,25},{17,1},{25,9},{2,18},{10... | collective-permute-start | bytes 3145736 | tf_op jit(solution)/shard_map/ppermute | solution.py:72
  264.6 33.0 %collective-permute-start.23 = (bf16[256,2048]{1,0:T(8,128)(2,1)}, bf16[256,2048]{1,0:T(8,128)(2,1)}, u32[]{:S(2)}, u32[]{:S(2)}) collective-permute-start(bf16[256,2048]{1,0:T(8,128)(2,1)} %pad_maximum_fusion.6), channel_id=1, source_target_pairs={{0,8},{8,0},{16,24},{24,16},{1,9},{9,1},{17,25},{25,17},{2,10},{10... | collective-permute-start | bytes 3145736 | tf_op jit(solution)/shard_map/ppermute | solution.py:72
  276.3 38.6 %collective-permute-start.17 = (bf16[256,2048]{1,0:T(8,128)(2,1)}, bf16[256,2048]{1,0:T(8,128)(2,1)}, u32[]{:S(2)}, u32[]{:S(2)}) collective-permute-start(bf16[256,2048]{1,0:T(8,128)(2,1)} %pad_maximum_fusion.5), channel_id=1, source_target_pairs={{0,16},{8,24},{16,0},{24,8},{1,17},{9,25},{17,1},{25,9},{2,18},{10... | collective-permute-start | bytes 3145736 | tf_op jit(solution)/shard_map/ppermute | solution.py:72
  277.7 38.7 %collective-permute-start.15 = (bf16[256,2048]{1,0:T(8,128)(2,1)}, bf16[256,2048]{1,0:T(8,128)(2,1)}, u32[]{:S(2)}, u32[]{:S(2)}) collective-permute-start(bf16[256,2048]{1,0:T(8,128)(2,1)} %pad_maximum_fusion.4), channel_id=1, source_target_pairs={{0,8},{8,0},{16,24},{24,16},{1,9},{9,1},{17,25},{25,17},{2,10},{10... | collective-permute-start | bytes 3145736 | tf_op jit(solution)/shard_map/ppermute | solution.py:72
  335.7 10.0 %all-to-all-start = ((bf16[4,256,256]{2,1,0:T(8,128)(2,1)}), bf16[4,256,256]{2,1,0:T(8,128)(2,1)S(1)}, u32[]{:S(2)}, u32[]{:S(2)}) async-start(bf16[4,256,256]{2,1,0:T(8,128)(2,1)} %bitcast.263), calls=%async_computation | async-start | bytes 1048576 | tf_op jit(solution)/shard_map/all_to_all | solution.py:227
  339.1 282.9 %reduce-scatter.5.cloned.1.call-start = ((), (), s32[]{:S(2)}) async-start(), calls=%async_computation.12 | async-start | bytes 1769472 | tf_op jit(solution)/shard_map/reduce_scatter | solution.py:211
  339.7 25.0 %copy-start.26 = (f32[4,1024]{1,0:T(4,128)}, f32[4,1024]{1,0:T(4,128)S(1)}, u32[]{:S(2)}) copy-start(f32[4,1024]{1,0:T(4,128)S(1)} %log_add_fusion) | copy-start | bytes 49156
  364.7 23.8 %copy-start.37 = (bf16[1024,32]{0,1:T(8,128)(2,1)S(1)}, bf16[1024,32]{0,1:T(8,128)(2,1)}, u32[]{:S(2)}) copy-start(bf16[1024,32]{0,1:T(8,128)(2,1)} %copy-done.36) | copy-start | bytes 196612
  388.5 31.2 %copy-start.15 = (f32[1024,32]{0,1:T(8,128)S(1)}, f32[1024,32]{0,1:T(8,128)}, u32[]{:S(2)}) copy-start(f32[1024,32]{0,1:T(8,128)} %copy-done.14) | copy-start | bytes 393220
  388.5 31.2 %copy-start.17 = (f32[1024,32]{0,1:T(8,128)S(1)}, f32[1024,32]{0,1:T(8,128)}, u32[]{:S(2)}) copy-start(f32[1024,32]{0,1:T(8,128)} %copy-done.16) | copy-start | bytes 393220
  388.5 32.7 %copy-start.24 = (f32[1024,4]{0,1:T(4,128)S(1)}, f32[1024,4]{0,1:T(4,128)}, u32[]{:S(2)}) copy-start(f32[1024,4]{0,1:T(4,128)} %copy-done.23) | copy-start | bytes 49156
  426.8 204.8 %reduce-scatter.9.cloned.1.call-start = ((), (), s32[]{:S(2)}) async-start(), calls=%async_computation.14 | async-start | bytes 9437184 | tf_op jit(solution)/shard_map/reduce_scatter | solution.py:211
  450.5 36.2 %copy-start.13 = (bf16[64,4,1024]{2,0,1:T(8,128)(2,1)S(1)}, bf16[64,4,1024]{2,0,1:T(8,128)(2,1)}, u32[]{:S(2)}) copy-start(bf16[64,4,1024]{2,0,1:T(8,128)(2,1)} %copy-done.12) | copy-start | bytes 1572868
  450.5 186.5 %reduce-scatter.7.cloned.1.call-start = ((), (), s32[]{:S(2)}) async-start(), calls=%async_computation.13 | async-start | bytes 1179648 | tf_op jit(solution)/shard_map/reduce_scatter | solution.py:231
  450.5 22.2 %collective-permute-start.31 = (bf16[256,2048]{1,0:T(8,128)(2,1)}, bf16[256,2048]{1,0:T(8,128)(2,1)S(1)}, u32[]{:S(2)}, u32[]{:S(2)}) collective-permute-start(bf16[256,2048]{1,0:T(8,128)(2,1)} %get-tuple-element.22), channel_id=1, source_target_pairs={{0,16},{8,24},{16,0},{24,8},{1,17},{9,25},{17,1},{25,9},{2,18},{10... | collective-permute-start | bytes 3145736 | tf_op jit(solution)/shard_map/ppermute | solution.py:72
  452.1 24.2 %collective-permute-start.30 = (bf16[256,2048]{1,0:T(8,128)(2,1)}, bf16[256,2048]{1,0:T(8,128)(2,1)S(1)}, u32[]{:S(2)}, u32[]{:S(2)}) collective-permute-start(bf16[256,2048]{1,0:T(8,128)(2,1)} %get-tuple-element.22), channel_id=1, source_target_pairs={{0,8},{8,0},{16,24},{24,16},{1,9},{9,1},{17,25},{25,17},{2,10},{10... | collective-permute-start | bytes 3145736 | tf_op jit(solution)/shard_map/ppermute | solution.py:72
  472.8 11.0 %collective-permute-start.33 = (bf16[128,2048]{1,0:T(8,128)(2,1)S(1)}, bf16[128,2048]{1,0:T(8,128)(2,1)S(1)}, u32[]{:S(2)}, u32[]{:S(2)}) collective-permute-start(bf16[128,2048]{1,0:T(8,128)(2,1)S(1)} %slice.215), channel_id=1, source_target_pairs={{0,8},{8,0},{16,24},{24,16},{1,9},{9,1},{17,25},{25,17},{2,10},{10... | collective-permute-start | bytes 1572872 | tf_op jit(solution)/shard_map/ppermute | solution.py:72
  476.4 9.2 %collective-permute-start.32 = (bf16[128,2048]{1,0:T(8,128)(2,1)S(1)}, bf16[128,2048]{1,0:T(8,128)(2,1)S(1)}, u32[]{:S(2)}, u32[]{:S(2)}) collective-permute-start(bf16[128,2048]{1,0:T(8,128)(2,1)S(1)} %slice.214), channel_id=1, source_target_pairs={{0,16},{8,24},{16,0},{24,8},{1,17},{9,25},{17,1},{25,9},{2,18},{10... | collective-permute-start | bytes 1572872 | tf_op jit(solution)/shard_map/ppermute | solution.py:72
  491.3 150.1 %reduce-scatter.11.cloned.1.call-start = ((), (), s32[]{:S(2)}) async-start(), calls=%async_computation.15 | async-start | bytes 4718592 | tf_op jit(solution)/shard_map/reduce_scatter | solution.py:202
  502.7 30.8 %collective-permute-start.27 = (bf16[2048,384]{1,0:T(8,128)(2,1)}, bf16[2048,384]{1,0:T(8,128)(2,1)}, u32[]{:S(2)}, u32[]{:S(2)}) collective-permute-start(bf16[2048,384]{1,0:T(8,128)(2,1)} %slice.188), channel_id=1, source_target_pairs={{0,16},{8,24},{16,0},{24,8},{1,17},{9,25},{17,1},{25,9},{2,18},{10... | collective-permute-start | bytes 4718600 | tf_op jit(solution)/shard_map/ppermute | solution.py:72
  502.8 33.0 %collective-permute-start.26 = (bf16[2048,384]{1,0:T(8,128)(2,1)}, bf16[2048,384]{1,0:T(8,128)(2,1)}, u32[]{:S(2)}, u32[]{:S(2)}) collective-permute-start(bf16[2048,384]{1,0:T(8,128)(2,1)} %slice.188), channel_id=1, source_target_pairs={{0,8},{8,0},{16,24},{24,16},{1,9},{9,1},{17,25},{25,17},{2,10},{10... | collective-permute-start | bytes 4718600 | tf_op jit(solution)/shard_map/ppermute | solution.py:72
  508.5 34.8 %copy-start.22 = (bf16[1024,1,64]{0,2,1:T(8,128)(2,1)S(1)}, bf16[1024,1,64]{0,2,1:T(8,128)(2,1)}, u32[]{:S(2)}) copy-start(bf16[1024,1,64]{0,2,1:T(8,128)(2,1)} %copy-done.21) | copy-start | bytes 393220
  535.7 19.0 %collective-permute-start.29 = (bf16[1024,384]{1,0:T(8,128)(2,1)}, bf16[1024,384]{1,0:T(8,128)(2,1)}, u32[]{:S(2)}, u32[]{:S(2)}) collective-permute-start(bf16[1024,384]{1,0:T(8,128)(2,1)} %slice.210), channel_id=1, source_target_pairs={{0,8},{8,0},{16,24},{24,16},{1,9},{9,1},{17,25},{25,17},{2,10},{10... | collective-permute-start | bytes 2359304 | tf_op jit(solution)/shard_map/ppermute | solution.py:72
  537.9 18.2 %collective-permute-start.28 = (bf16[1024,384]{1,0:T(8,128)(2,1)}, bf16[1024,384]{1,0:T(8,128)(2,1)}, u32[]{:S(2)}, u32[]{:S(2)}) collective-permute-start(bf16[1024,384]{1,0:T(8,128)(2,1)} %slice.209), channel_id=1, source_target_pairs={{0,16},{8,24},{16,0},{24,8},{1,17},{9,25},{17,1},{25,9},{2,18},{10... | collective-permute-start | bytes 2359304 | tf_op jit(solution)/shard_map/ppermute | solution.py:72
  545.2 14.0 %all-to-all-start.1 = ((bf16[4,256,384]{2,1,0:T(8,128)(2,1)}), bf16[4,256,384]{2,1,0:T(8,128)(2,1)S(1)}, u32[]{:S(2)}, u32[]{:S(2)}) async-start(bf16[4,256,384]{2,1,0:T(8,128)(2,1)} %pad_maximum_fusion.8), calls=%async_computation.1 | async-start | bytes 1572864 | tf_op jit(solution)/shard_map/all_to_all | solution.py:247
  622.1 9.6 %all-to-all-start.2 = ((bf16[4,64,384]{2,1,0:T(8,128)(2,1)}), bf16[4,64,384]{2,1,0:T(8,128)(2,1)S(1)}, u32[]{:S(2)}, u32[]{:S(2)}) async-start(bf16[4,64,384]{2,1,0:T(8,128)(2,1)} %bitcast.286), calls=%async_computation.3 | async-start | bytes 393216 | tf_op jit(solution)/shard_map/all_to_all | solution.py:213
  631.7 15.7 %all-to-all-start.3 = ((bf16[4,64,2048]{2,1,0:T(8,128)(2,1)}), bf16[4,64,2048]{2,1,0:T(8,128)(2,1)S(1)}, u32[]{:S(2)}, u32[]{:S(2)}) async-start(bf16[4,64,2048]{2,1,0:T(8,128)(2,1)} %bitcast.280), calls=%async_computation.6 | async-start | bytes 2097152 | tf_op jit(solution)/shard_map/all_to_all | solution.py:213
  (37 other events, 240.8 us)
Sparse Core Ops, SparseCore 0:
  10.2 43.0 all-gather.6
  55.5 30.0 all-gather.4
  87.8 81.5 all-gather.8
  170.8 45.6 all-gather.10
  427.0 39.8 reduce-scatter.4
  469.0 87.4 reduce-scatter.8
  559.4 30.5 reduce-scatter.6
  592.2 49.0 reduce-scatter.10
where the time goes:
time: 667 us; the launch traced here: 657 us
  matrix products  184 us (28%)
  waiting for transfers between devices  170 us (25%)
  local copies, waits for them, and re-layouts  87.9 us (13%)
  starting transfers between devices  79.1 us (12%)
  other arithmetic  67.2 us (10%)
  blocking collectives  52.6 us (8%)
  between operations  15.6 us (2%)
    ppermute x32, waiting for transfers between devices, swap(): return lax.ppermute(value, 'sp', [(i, i ^ mask) for i in range(count)])  153 us
    ppermute x32, starting transfers between devices, swap(): return lax.ppermute(value, 'sp', [(i, i ^ mask) for i in range(count)])  60.9 us
    psum x1, blocking collectives, local(): tiny = lax.psum(tiny, ('sp', 'fsdp'))  52.6 us
    dot_general x3, matrix products, times_transposed(): lax.dot_general(a, b, (((1,), (1,)), ((), ())), preferred_element_type=f32)  30.9 us
    dot_general x4, matrix products, over_rows(): lax.dot_general(a, b, (((0,), (0,)), ((), ())), preferred_element_type=f32)  30.7 us
    dynamic_update_slice x17, local copies, waits for them, and re-layouts, gather_chunks(): stack = lax.dynamic_update_slice_in_dim(stack, part[None], s ^ mask, 0)  27.5 us
    dot_general x1, matrix products, attend_back(): jnp.einsum('gqt,td->qgd', grad_s, k, preferred_element_type=f32) * scale  27 us
    dot_general x1, matrix products, attend_back(): jnp.einsum('gqt,qgd->td', grad_s, q, preferred_element_type=f32) * scale  23.8 us
  transfers between devices with their start and end apart: 46, of which 25 were waited for; matrix products, arithmetic and copies ran while one was open for 31% of the time, Pallas kernels for 0%

commit v1 on v0

--- a/solution.py
+++ b/solution.py
@@ -251,7 +251,7 @@
     grad_x, grad_g_attn = attn_pull(grad_normed)
     grad_input = grad_middle + grad_x
     tiny = jnp.concatenate([grad_g_attn, grad_g_ffn, grad_g_query, grad_g_key])
-    tiny = lax.psum(tiny, ("sp", "fsdp"))
+    tiny = lax.psum(lax.psum(tiny, "fsdp"), "sp")
     mine = (s * F + lax.axis_index("fsdp")) * rows_d
     return (
         out[None],

time: 667 us -> 663 us (level)
    psum x1 -> x2, blocking collectives: 52.6 us -> 52.2 us  [local(): tiny = lax.psum(lax.psum(tiny, 'fsdp'), 'sp')]
where the time goes in v1:
time: 663 us; the launch traced here: 653 us
  matrix products  184 us (28%)
  waiting for transfers between devices  168 us (25%)
  local copies, waits for them, and re-layouts  87.8 us (13%)
  starting transfers between devices  77.8 us (12%)
  other arithmetic  67.1 us (10%)
  blocking collectives  52.2 us (8%)
  between operations  15.6 us (2%)
    ppermute x32, waiting for transfers between devices, swap(): return lax.ppermute(value, 'sp', [(i, i ^ mask) for i in range(count)])  154 us
    ppermute x32, starting transfers between devices, swap(): return lax.ppermute(value, 'sp', [(i, i ^ mask) for i in range(count)])  60.7 us
    psum x2, blocking collectives, local(): tiny = lax.psum(lax.psum(tiny, 'fsdp'), 'sp')  52.2 us
    dot_general x3, matrix products, times_transposed(): lax.dot_general(a, b, (((1,), (1,)), ((), ())), preferred_element_type=f32)  30.9 us
    dot_general x4, matrix products, over_rows(): lax.dot_general(a, b, (((0,), (0,)), ((), ())), preferred_element_type=f32)  30.8 us
    dynamic_update_slice x17, local copies, waits for them, and re-layouts, gather_chunks(): stack = lax.dynamic_update_slice_in_dim(stack, part[None], s ^ mask, 0)  27.4 us
    dot_general x1, matrix products, attend_back(): jnp.einsum('gqt,td->qgd', grad_s, k, preferred_element_type=f32) * scale  27.3 us
    dot_general x1, matrix products, attend_back(): jnp.einsum('gqt,qgd->td', grad_s, q, preferred_element_type=f32) * scale  23.8 us
  transfers between devices with their start and end apart: 46, of which 25 were waited for; matrix products, arithmetic and copies ran while one was open for 31% of the time, Pallas kernels for 0%

profile of v1, /device:TPU:0, one launch (start us, length us, event | category | flops | bytes accessed | tf_op | source)
XLA Modules:
  0.0 652.9 jit_solution(2754737519687339180)
XLA Ops:
  16.5 11.6 %collective-permute-start = (bf16[256,2048]{1,0:T(8,128)(2,1)S(1)}, bf16[256,2048]{1,0:T(8,128)(2,1)}, u32[]{:S(2)}, u32[]{:S(2)}) collective-permute-start(bf16[256,2048]{1,0:T(8,128)(2,1)S(1)} %bitcast.265), channel_id=1, source_target_pairs={{0,8},{8,0},{16,24},{24,16},{1,9},{9,1},{17,25},{25,17},{2,10},{10... | collective-permute-start | bytes 3145736 | tf_op jit(solution)/shard_map/ppermute | solution.py:72
  28.2 3.7 collective-permute-start.1
  34.7 2.6 broadcast.254.clone.1
  38.3 2.5 broadcast.254.clone.2
  44.9 21.8 %collective-permute-done.1 = bf16[256,2048]{1,0:T(8,128)(2,1)} collective-permute-done((bf16[256,2048]{1,0:T(8,128)(2,1)S(1)}, bf16[256,2048]{1,0:T(8,128)(2,1)}, u32[]{:S(2)}, u32[]{:S(2)}) %collective-permute-start.1) | collective-permute-done | bytes 1048608 | tf_op jit(solution)/shard_map/ppermute | solution.py:72
  67.8 16.5 %collective-permute-start.3 = (bf16[128,2048]{1,0:T(8,128)(2,1)S(1)}, bf16[128,2048]{1,0:T(8,128)(2,1)S(1)}, u32[]{:S(2)}, u32[]{:S(2)}) collective-permute-start(bf16[128,2048]{1,0:T(8,128)(2,1)S(1)} %slice.186), channel_id=1, source_target_pairs={{0,8},{8,0},{16,24},{24,16},{1,9},{9,1},{17,25},{25,17},{2,10},{10... | collective-permute-start | bytes 1572872 | tf_op jit(solution)/shard_map/ppermute | solution.py:72
  90.8 2.5 collective-permute-start.20
  93.3 2.4 bitcast_dynamic-update-slice_fusion.12
  95.7 2.4 bitcast_dynamic-update-slice_fusion.7
  98.0 2.3 bitcast_dynamic-update-slice_fusion.11
  100.4 2.3 bitcast_dynamic-update-slice_fusion.6
  105.6 3.1 fusion.8
  108.8 2.7 collective-permute-done.20
  113.6 2.6 broadcast.254.clone
  117.3 16.3 %collective-permute-done.10 = bf16[256,2048]{1,0:T(8,128)(2,1)S(1)} collective-permute-done((bf16[256,2048]{1,0:T(8,128)(2,1)}, bf16[256,2048]{1,0:T(8,128)(2,1)S(1)}, u32[]{:S(2)}, u32[]{:S(2)}) %collective-permute-start.10) | collective-permute-done | bytes 1048608 | tf_op jit(solution)/shard_map/ppermute | solution.py:72
  138.6 3.3 fusion.10
  145.9 7.9 %fusion.108 = (f32[4,1024]{1,0:T(4,128)S(1)}, f32[4,1024,1024]{1,2,0:T(8,128)}) fusion(bf16[1024,4,32]{0,2,1:T(8,128)(2,1)S(1)} %get-tuple-element.39, bf16[1024,4,32]{0,2,1:T(8,128)(2,1)S(1)} %get-tuple-element.38, bf16[1024,32]{0,1:T(8,128)(2,1)S(1)} %get-tuple-element.51, bf16[1024,32]{0,1:T(8,128)(2,1)S(1)} %get-tuple-element.50, ...), kind=kOutput, calls=%fused_computation.228 | convolution fusion | flops 550760448 | bytes 18497536 | tf_op jit(solution)/shard_map/qgd,td->gqt/dot_general | solution.py:41
  153.8 8.1 %fusion.4 = f32[4,1024]{1,0:T(4,128)S(1)} fusion(f32[4,1024,1024]{1,2,0:T(8,128)} %get-tuple-element.61, f32[4,1024]{1,0:T(4,128)S(1)} %get-tuple-element.60), kind=kLoop, calls=%fused_computation.10 | loop fusion | flops 8384512 | bytes 16809984 | tf_op jit(solution)/shard_map/reduce_sum | solution.py:52
  161.9 7.5 %fusion.35 = bf16[64,4,1024]{2,0,1:T(8,128)(2,1)S(1)} fusion(f32[4,1024,1024]{1,2,0:T(8,128)} %get-tuple-element.61, f32[4,1024]{1,0:T(4,128)S(1)} %fusion.4, f32[4,1024]{1,0:T(4,128)S(1)} %get-tuple-element.60, f32[1024,384]{0,1:T(8,128)S(1)} %fusion.100), kind=kOutput, calls=%fused_computation.76 | convolution fusion | flops 549715968 | bytes 17465344 | tf_op jit(solution)/shard_map/gqt,td->qgd/dot_general | solution.py:54
  175.3 2.3 fusion.54
  178.0 8.0 %collective-permute-done.5 = bf16[1024,256]{1,0:T(8,128)(2,1)} collective-permute-done((bf16[1024,256]{1,0:T(8,128)(2,1)}, bf16[1024,256]{1,0:T(8,128)(2,1)}, u32[]{:S(2)}, u32[]{:S(2)}) %collective-permute-start.5) | collective-permute-done | bytes 524320 | tf_op jit(solution)/shard_map/ppermute | solution.py:72
  195.2 9.9 %multiply_reduce_fusion = (f32[1024]{0:T(1024)S(1)}, f32[1024,2048]{1,0:T(8,128)}) fusion(bf16[4,256,2048]{2,1,0:T(8,128)(2,1)} %fusion.54, bf16[4,1024,256]{2,1,0:T(8,128)(2,1)S(1)} %fusion.62, bf16[4,256,2048]{2,1,0:T(8,128)(2,1)} %fusion.53), kind=kOutput, calls=%fused_computation.22 | convolution fusion | flops 4303354880 | bytes 18878464 | tf_op jit(solution)/shard_map/dot_general | solution.py:191
  205.1 15.9 %fusion.102 = f32[1024,2048]{1,0:T(8,128)} fusion(bf16[2048,2048]{1,0:T(8,128)(2,1)} %all-gather.9.cloned.1.call-done, f32[1024,2048]{1,0:T(8,128)} %get-tuple-element.63, f32[2048]{0:T(1024)S(1)} %get-tuple-element.15, f32[1024]{0:T(1024)S(1)} %add_rsqrt_fusion), kind=kOutput, calls=%fused_computation.223 | convolution fusion | flops 8596226048 | bytes 25178112 | tf_op jit(solution)/shard_map/dot_general | solution.py:193
  221.0 14.7 %fusion.18 = (bf16[1024,1024]{1,0:T(8,128)(2,1)}, bf16[1024,1024]{1,0:T(8,128)(2,1)}, bf16[1024,1024]{1,0:T(8,128)(2,1)}) fusion(f32[1024,2048]{1,0:T(8,128)} %fusion.102, bf16[1024,2048]{1,0:T(8,128)(2,1)} %bitcast.31, bf16[1024,2048]{1,0:T(8,128)(2,1)} %all-gather.11.cloned.1.call-done), kind=kOutput, calls=%fused_computation.30 | convolution fusion | flops 4311744512 | bytes 23068672 | tf_op jit(solution)/shard_map/dot_general | solution.py:36
  235.7 10.9 %fusion.21 = f32[1024,2048]{1,0:T(8,128)S(1)} fusion(bf16[2048,2048]{1,0:T(8,128)(2,1)S(1)} %copy-done.50, bf16[1024,1024]{1,0:T(8,128)(2,1)} %get-tuple-element.25, bf16[1024,1024]{1,0:T(8,128)(2,1)} %get-tuple-element.24), kind=kOutput, calls=%fused_computation.48 | convolution fusion | flops 8598323200 | bytes 20971520 | tf_op jit(solution)/shard_map/dot_general | solution.py:36
  249.7 2.2 copy-done.51
  251.9 6.1 fusion.109
  265.4 7.7 %collective-permute-done.14 = bf16[128,2048]{1,0:T(8,128)(2,1)S(1)} collective-permute-done((bf16[128,2048]{1,0:T(8,128)(2,1)S(1)}, bf16[128,2048]{1,0:T(8,128)(2,1)S(1)}, u32[]{:S(2)}, u32[]{:S(2)}) %collective-permute-start.14) | collective-permute-done | bytes 524320 | tf_op jit(solution)/shard_map/ppermute | solution.py:72
  280.7 14.9 %collective-permute-done.25 = bf16[256,2048]{1,0:T(8,128)(2,1)S(1)} collective-permute-done((bf16[256,2048]{1,0:T(8,128)(2,1)}, bf16[256,2048]{1,0:T(8,128)(2,1)S(1)}, u32[]{:S(2)}, u32[]{:S(2)}) %collective-permute-start.25) | collective-permute-done | bytes 1048608 | tf_op jit(solution)/shard_map/ppermute | solution.py:72
  297.4 17.4 %collective-permute-done.17 = bf16[256,2048]{1,0:T(8,128)(2,1)} collective-permute-done((bf16[256,2048]{1,0:T(8,128)(2,1)}, bf16[256,2048]{1,0:T(8,128)(2,1)}, u32[]{:S(2)}, u32[]{:S(2)}) %collective-permute-start.17) | collective-permute-done | bytes 1048608 | tf_op jit(solution)/shard_map/ppermute | solution.py:72
  316.3 6.6 %multiply_reduce_fusion.1 = (f32[2048]{0:T(1024)}, f32[256]{0:T(256)S(1)}, bf16[1,256,2048]{2,1,0:T(8,128)(2,1)}) fusion(f32[1024,2048]{1,0:T(8,128)} %get-tuple-element.63, s32[]{:T(128)S(6)} %select_n.92, f32[256]{0:T(256)S(1)} %fusion.90, bf16[256,2048]{1,0:T(8,128)(2,1)S(1)} %collective-permute-done.25, bf16[256,2048]{1,0:T(8,128)(2,1)} %collective-permute-done.23, ...), kind=kLoop, calls=%fused_computation.58 | loop fusion | flops 8386304 | bytes 11552772 | tf_op jit(solution)/shard_map/transpose(jvp())/reduce_sum | solution.py:15
  324.1 5.3 bitcast_dynamic-update-slice_fusion.5
  329.4 5.3 convolution_convert_fusion.4
  335.5 3.5 all-to-all-start
  339.6 6.0 all-to-all-done
  348.0 8.1 %fusion.85 = f32[1024,1024,4]{1,0,2:T(8,128)} fusion(bf16[1024,4,64]{0,2,1:T(8,128)(2,1)S(1)} %reshape.378, f32[1024,384]{0,1:T(8,128)S(1)} %fusion.100), kind=kOutput, calls=%fused_computation.185 | convolution fusion | flops 536870912 | bytes 17432576 | tf_op jit(solution)/shard_map/qgd,td->gqt/dot_general | solution.py:62
  356.1 8.4 %fusion.42 = bf16[1024,64]{0,1:T(8,128)(2,1)S(1)} fusion(bf16[1024,4,64]{0,2,1:T(8,128)(2,1)S(1)} %reshape.378, f32[4,1024,1024]{1,2,0:T(8,128)} %get-tuple-element.61, f32[4,1024]{1,0:T(4,128)S(1)} %log_add_fusion), kind=kOutput, calls=%fused_computation.81 | convolution fusion | flops 545325056 | bytes 17448960 | tf_op jit(solution)/shard_map/gqt,qgd->td/dot_general | solution.py:61
  364.6 23.8 %fusion.46 = f32[1024,1,64]{0,2,1:T(8,128)S(1)} fusion(f32[1024,1024,4]{1,0,2:T(8,128)} %fusion.85, f32[4,1024,1024]{1,2,0:T(8,128)} %get-tuple-element.61, f32[4,1024]{1,0:T(4,128)S(1)} %log_add_fusion, pred[1024,1024]{0,1:T(8,128)(4,1)} %fusion.20, bf16[1024,4,32]{0,2,1:T(8,128)(2,1)} %copy-done.25, bf16[1024,4,32]{0,2,1:T(8,128)(2,1)S(1)} %get-tuple-element.38), kind=kOutput, calls=%fused_computation.83 | convolution fusion | flops 567481344 | bytes 35405824 | tf_op jit(solution)/shard_map/gqt,qgd->td/dot_general | solution.py:67
  388.4 27.3 %fusion.34 = f32[1024,4,64]{0,2,1:T(8,128)} fusion(f32[1024,1024,4]{1,0,2:T(8,128)} %fusion.85, f32[4,1024,1024]{1,2,0:T(8,128)} %get-tuple-element.61, f32[4,1024]{1,0:T(4,128)} %copy-done.26, pred[1024,1024]{0,1:T(8,128)(4,1)} %fusion.20, bf16[1024,32]{0,1:T(8,128)(2,1)S(1)} %copy-done.39, bf16[1024,32]{0,1:T(8,128)(2,1)S(1)} %copy-done.37), kind=kOutput, calls=%fused_computation.74 | convolution fusion | flops 567284736 | bytes 35799040 | tf_op jit(solution)/shard_map/gqt,td->qgd/dot_general | solution.py:66
  423.1 2.5 convolution_convert_fusion.2
  427.1 15.1 %convolution_convert_fusion = bf16[2048,2048]{1,0:T(8,128)(2,1)} fusion(bf16[1024,1024]{1,0:T(8,128)(2,1)} %get-tuple-element.25, bf16[1024,1024]{1,0:T(8,128)(2,1)} %get-tuple-element.24, f32[1024,2048]{1,0:T(8,128)} %get-tuple-element.63, f32[2048]{0:T(1024)S(1)} %copy-done.33, f32[1024]{0:T(1024)S(1)} %copy-done.48), kind=kOutput, calls=%fused_computation.26 | convolution fusion | flops 8608808960 | bytes 20983808 | tf_op jit(solution)/shard_map/dot_general | solution.py:32
  442.2 8.4 %copy.92 = bf16[4,8,64,2048]{3,2,0,1:T(8,128)(2,1)} copy(bf16[4,8,64,2048]{3,2,1,0:T(8,128)(2,1)} %bitcast.267) | data formatting | bytes 16777216 | tf_op jit(solution)/shard_map/reshape | solution.py:209
  452.8 20.2 %collective-permute-done.31 = bf16[256,2048]{1,0:T(8,128)(2,1)S(1)} collective-permute-done((bf16[256,2048]{1,0:T(8,128)(2,1)}, bf16[256,2048]{1,0:T(8,128)(2,1)S(1)}, u32[]{:S(2)}, u32[]{:S(2)}) %collective-permute-start.31) | collective-permute-done | bytes 1048608 | tf_op jit(solution)/shard_map/ppermute | solution.py:72
  473.0 2.2 collective-permute-start.33
  478.8 5.2 collective-permute-done.33
  486.8 4.6 convolution_convert_fusion.3
  491.5 8.6 %convolution_convert_fusion.1 = bf16[1024,2048]{1,0:T(8,128)(2,1)} fusion(bf16[1024,1024]{1,0:T(8,128)(2,1)S(1)} %copy-done.54, bf16[1024,2048]{1,0:T(8,128)(2,1)} %bitcast.31), kind=kOutput, calls=%fused_computation.39 | convolution fusion | flops 4297064448 | bytes 10485760 | tf_op jit(solution)/shard_map/dot_general | solution.py:32
  500.1 2.8 slice.188
  505.4 3.2 broadcast_in_dim.152
  508.6 2.8 bitcast_dynamic-update-slice_fusion.2
  511.4 22.4 %collective-permute-done.27 = bf16[2048,384]{1,0:T(8,128)(2,1)} collective-permute-done((bf16[2048,384]{1,0:T(8,128)(2,1)}, bf16[2048,384]{1,0:T(8,128)(2,1)}, u32[]{:S(2)}, u32[]{:S(2)}) %collective-permute-start.27) | collective-permute-done | bytes 1572896 | tf_op jit(solution)/shard_map/ppermute | solution.py:72
  538.2 2.3 collective-permute-start.28
  540.5 2.7 bitcast_dynamic-update-slice_fusion.1
  545.3 3.6 all-to-all-start.1
  549.0 2.8 bitcast_dynamic-update-slice_fusion
  551.8 3.2 collective-permute-done.29
  556.4 2.7 fusion.30
  559.5 6.0 fusion.28
  565.7 36.6 %psum.14 = f32[4224]{0:T(1024)S(1)} all-reduce(f32[4224]{0:T(1024)S(1)} %concatenate.101), channel_id=1, replica_groups=mesh['sp'=4,'fsdp'=8] {'fsdp'}, use_global_device_ids=true, to_apply=%region_21.22 | all-reduce | flops 4224 | bytes 33792 | tf_op jit(solution)/shard_map/psum | solution.py:254
  602.3 15.6 %psum.15 = f32[4224]{0:T(1024)S(1)} all-reduce(f32[4224]{0:T(1024)S(1)} %psum.14), channel_id=1, replica_groups=mesh['sp'=4,'fsdp'=8] {'sp'}, use_global_device_ids=true, to_apply=%region_22.23 | all-reduce | flops 4224 | bytes 33792 | tf_op jit(solution)/shard_map/psum | solution.py:254
  617.9 4.1 fusion.24
  622.0 3.4 all-to-all-start.2
  625.4 5.2 all-to-all-done.2
  630.5 3.5 all-to-all-start.3
  (301 shorter events, 121.1 us)
Async XLA Ops:
  7.2 24.9 %copy-start = (bf16[512,2048]{1,0:T(8,128)(2,1)S(1)}, bf16[512,2048]{1,0:T(8,128)(2,1)}, u32[]{:S(2)}) copy-start(bf16[512,2048]{1,0:T(8,128)(2,1)} %param.19) | copy-start | bytes 6291460
  7.2 27.4 %copy-start.52 = (bf16[64]{0:T(256)(128)(2,1)S(1)}, bf16[64]{0:T(256)(128)(2,1)}, u32[]{:S(2)}) copy-start(bf16[64]{0:T(256)(128)(2,1)} %param.22) | copy-start | bytes 388
  7.2 27.4 %copy-start.42 = (s32[1,1024]{1,0:T(1,128)S(1)}, s32[1,1024]{1,0:T(1,128)}, u32[]{:S(2)}) copy-start(s32[1,1024]{1,0:T(1,128)} %param.13) | copy-start | bytes 12292
  7.2 27.4 %copy-start.53 = (bf16[64]{0:T(256)(128)(2,1)S(1)}, bf16[64]{0:T(256)(128)(2,1)}, u32[]{:S(2)}) copy-start(bf16[64]{0:T(256)(128)(2,1)} %param.23) | copy-start | bytes 388
  7.2 96.6 %all-gather.7.cloned.1.call-start = ((), (), s32[]{:S(2)}) async-start(), calls=%async_computation.9 | async-start | bytes 1179648 | tf_op jit(solution)/shard_map/all_gather | solution.py:149
  8.4 0.7 collective-permute-start.8
  9.8 127.0 %all-gather.5.cloned.1.call-start = ((), (), s32[]{:S(2)}) async-start(), calls=%async_computation.8 | async-start | bytes 2359296 | tf_op jit(solution)/shard_map/all_gather | solution.py:149
  14.1 191.1 %all-gather.9.cloned.1.call-start = ((), (), s32[]{:S(2)}) async-start(), calls=%async_computation.10 | async-start | bytes 9437184 | tf_op jit(solution)/shard_map/all_gather | solution.py:149
  16.5 204.5 %all-gather.11.cloned.1.call-start = ((), (), s32[]{:S(2)}) async-start(), calls=%async_computation.11 | async-start | bytes 4718592 | tf_op jit(solution)/shard_map/all_gather | solution.py:149
  16.5 67.8 %collective-permute-start = (bf16[256,2048]{1,0:T(8,128)(2,1)S(1)}, bf16[256,2048]{1,0:T(8,128)(2,1)}, u32[]{:S(2)}, u32[]{:S(2)}) collective-permute-start(bf16[256,2048]{1,0:T(8,128)(2,1)S(1)} %bitcast.265), channel_id=1, source_target_pairs={{0,8},{8,0},{16,24},{24,16},{1,9},{9,1},{17,25},{25,17},{2,10},{10... | collective-permute-start | bytes 3145736 | tf_op jit(solution)/shard_map/ppermute | solution.py:72
  28.2 38.6 %collective-permute-start.1 = (bf16[256,2048]{1,0:T(8,128)(2,1)S(1)}, bf16[256,2048]{1,0:T(8,128)(2,1)}, u32[]{:S(2)}, u32[]{:S(2)}) collective-permute-start(bf16[256,2048]{1,0:T(8,128)(2,1)S(1)} %bitcast.266), channel_id=1, source_target_pairs={{0,16},{8,24},{16,0},{24,8},{1,17},{9,25},{17,1},{25,9},{2,18},{10... | collective-permute-start | bytes 3145736 | tf_op jit(solution)/shard_map/ppermute | solution.py:72
  31.9 57.0 %collective-permute-start.18 = (bf16[256,2048]{1,0:T(8,128)(2,1)}, bf16[256,2048]{1,0:T(8,128)(2,1)}, u32[]{:S(2)}, u32[]{:S(2)}) collective-permute-start(bf16[256,2048]{1,0:T(8,128)(2,1)} %bitcast.269), channel_id=1, source_target_pairs={{0,8},{8,0},{16,24},{24,16},{1,9},{9,1},{17,25},{25,17},{2,10},{10... | collective-permute-start | bytes 3145736 | tf_op jit(solution)/shard_map/ppermute | solution.py:72
  32.0 54.7 %collective-permute-start.19 = (bf16[256,2048]{1,0:T(8,128)(2,1)}, bf16[256,2048]{1,0:T(8,128)(2,1)}, u32[]{:S(2)}, u32[]{:S(2)}) collective-permute-start(bf16[256,2048]{1,0:T(8,128)(2,1)} %bitcast.270), channel_id=1, source_target_pairs={{0,16},{8,24},{16,0},{24,8},{1,17},{9,25},{17,1},{25,9},{2,18},{10... | collective-permute-start | bytes 3145736 | tf_op jit(solution)/shard_map/ppermute | solution.py:72
  32.9 11.2 %collective-permute-start.13 = (bf16[128,2048]{1,0:T(8,128)(2,1)}, bf16[128,2048]{1,0:T(8,128)(2,1)S(1)}, u32[]{:S(2)}, u32[]{:S(2)}) collective-permute-start(bf16[128,2048]{1,0:T(8,128)(2,1)} %constant_dynamic-slice_fusion), channel_id=1, source_target_pairs={{0,0},{1,4},{2,8},{3,12},{4,16},{5,20},{6,24},{7,28},{8,1},{9,5},{... | collective-permute-start | bytes 1572872 | tf_op jit(solution)/shard_map/ppermute | solution.py:146
  34.6 110.8 %copy-start.43 = (f32[64]{0:T(128)}, f32[64]{0:T(128)S(1)}, u32[]{:S(2)}) copy-start(f32[64]{0:T(128)S(1)} %convert_element_type.196) | copy-start | bytes 772
  34.6 110.2 %copy-start.34 = (f32[1024]{0:T(1024)}, f32[1024]{0:T(1024)S(1)}, u32[]{:S(2)}) copy-start(f32[1024]{0:T(1024)S(1)} %convert_element_type.195) | copy-start | bytes 12292
  34.6 110.0 %copy-start.46 = (f32[64]{0:T(128)}, f32[64]{0:T(128)S(1)}, u32[]{:S(2)}) copy-start(f32[64]{0:T(128)S(1)} %convert_element_type.194) | copy-start | bytes 772
  34.7 110.1 %copy-start.45 = (f32[32]{0:T(128)}, f32[32]{0:T(128)S(1)}, u32[]{:S(2)}) copy-start(f32[32]{0:T(128)S(1)} %multiply_power_fusion) | copy-start | bytes 388
  42.4 103.2 %copy-start.14 = (f32[1024,32]{0,1:T(8,128)}, f32[1024,32]{0,1:T(8,128)S(1)}, u32[]{:S(2)}) copy-start(f32[1024,32]{0,1:T(8,128)S(1)} %get-tuple-element.58) | copy-start | bytes 393220
  42.4 103.2 %copy-start.16 = (f32[1024,32]{0,1:T(8,128)}, f32[1024,32]{0,1:T(8,128)S(1)}, u32[]{:S(2)}) copy-start(f32[1024,32]{0,1:T(8,128)S(1)} %get-tuple-element.59) | copy-start | bytes 393220
  67.8 34.9 %collective-permute-start.3 = (bf16[128,2048]{1,0:T(8,128)(2,1)S(1)}, bf16[128,2048]{1,0:T(8,128)(2,1)S(1)}, u32[]{:S(2)}, u32[]{:S(2)}) collective-permute-start(bf16[128,2048]{1,0:T(8,128)(2,1)S(1)} %slice.186), channel_id=1, source_target_pairs={{0,8},{8,0},{16,24},{24,16},{1,9},{9,1},{17,25},{25,17},{2,10},{10... | collective-permute-start | bytes 1572872 | tf_op jit(solution)/shard_map/ppermute | solution.py:72
  85.4 17.3 %collective-permute-start.2 = (bf16[128,2048]{1,0:T(8,128)(2,1)S(1)}, bf16[128,2048]{1,0:T(8,128)(2,1)S(1)}, u32[]{:S(2)}, u32[]{:S(2)}) collective-permute-start(bf16[128,2048]{1,0:T(8,128)(2,1)S(1)} %slice.185), channel_id=1, source_target_pairs={{0,16},{8,24},{16,0},{24,8},{1,17},{9,25},{17,1},{25,9},{2,18},{10... | collective-permute-start | bytes 1572872 | tf_op jit(solution)/shard_map/ppermute | solution.py:72
  88.6 20.2 %collective-permute-start.21 = (bf16[128,2048]{1,0:T(8,128)(2,1)}, bf16[128,2048]{1,0:T(8,128)(2,1)S(1)}, u32[]{:S(2)}, u32[]{:S(2)}) collective-permute-start(bf16[128,2048]{1,0:T(8,128)(2,1)} %slice.206), channel_id=1, source_target_pairs={{0,8},{8,0},{16,24},{24,16},{1,9},{9,1},{17,25},{25,17},{2,10},{10... | collective-permute-start | bytes 1572872 | tf_op jit(solution)/shard_map/ppermute | solution.py:72
  90.8 20.7 %collective-permute-start.20 = (bf16[128,2048]{1,0:T(8,128)(2,1)}, bf16[128,2048]{1,0:T(8,128)(2,1)}, u32[]{:S(2)}, u32[]{:S(2)}) collective-permute-start(bf16[128,2048]{1,0:T(8,128)(2,1)} %slice.205), channel_id=1, source_target_pairs={{0,16},{8,24},{16,0},{24,8},{1,17},{9,25},{17,1},{25,9},{2,18},{10... | collective-permute-start | bytes 1572872 | tf_op jit(solution)/shard_map/ppermute | solution.py:72
  103.8 30.6 %collective-permute-start.9 = (bf16[256,2048]{1,0:T(8,128)(2,1)}, bf16[256,2048]{1,0:T(8,128)(2,1)S(1)}, u32[]{:S(2)}, u32[]{:S(2)}) collective-permute-start(bf16[256,2048]{1,0:T(8,128)(2,1)} %all-gather.7.cloned.1.call-done), channel_id=1, source_target_pairs={{0,8},{8,0},{16,24},{24,16},{1,9},{9,1},{17,25},{25,17},{2,10},{10... | collective-permute-start | bytes 3145736 | tf_op jit(solution)/shard_map/ppermute | solution.py:72
  105.5 28.1 %collective-permute-start.10 = (bf16[256,2048]{1,0:T(8,128)(2,1)}, bf16[256,2048]{1,0:T(8,128)(2,1)S(1)}, u32[]{:S(2)}, u32[]{:S(2)}) collective-permute-start(bf16[256,2048]{1,0:T(8,128)(2,1)} %all-gather.7.cloned.1.call-done), channel_id=1, source_target_pairs={{0,16},{8,24},{16,0},{24,8},{1,17},{9,25},{17,1},{25,9},{2,18},{10... | collective-permute-start | bytes 3145736 | tf_op jit(solution)/shard_map/ppermute | solution.py:72
  134.4 40.8 %collective-permute-start.12 = (bf16[128,2048]{1,0:T(8,128)(2,1)}, bf16[128,2048]{1,0:T(8,128)(2,1)}, u32[]{:S(2)}, u32[]{:S(2)}) collective-permute-start(bf16[128,2048]{1,0:T(8,128)(2,1)} %slice.199), channel_id=1, source_target_pairs={{0,8},{8,0},{16,24},{24,16},{1,9},{9,1},{17,25},{25,17},{2,10},{10... | collective-permute-start | bytes 1572872 | tf_op jit(solution)/shard_map/ppermute | solution.py:72
  135.2 40.0 %collective-permute-start.11 = (bf16[128,2048]{1,0:T(8,128)(2,1)}, bf16[128,2048]{1,0:T(8,128)(2,1)}, u32[]{:S(2)}, u32[]{:S(2)}) collective-permute-start(bf16[128,2048]{1,0:T(8,128)(2,1)} %slice.198), channel_id=1, source_target_pairs={{0,16},{8,24},{16,0},{24,8},{1,17},{9,25},{17,1},{25,9},{2,18},{10... | collective-permute-start | bytes 1572872 | tf_op jit(solution)/shard_map/ppermute | solution.py:72
  138.6 184.9 %copy-start.32 = (f32[2048]{0:T(1024)}, f32[2048]{0:T(1024)S(1)}, u32[]{:S(2)}) copy-start(f32[2048]{0:T(1024)S(1)} %get-tuple-element.15) | copy-start | bytes 24580
  170.4 17.0 %collective-permute-start.4 = (bf16[1024,256]{1,0:T(8,128)(2,1)}, bf16[1024,256]{1,0:T(8,128)(2,1)}, u32[]{:S(2)}, u32[]{:S(2)}) collective-permute-start(bf16[1024,256]{1,0:T(8,128)(2,1)} %copy.76), channel_id=1, source_target_pairs={{0,8},{8,0},{16,24},{24,16},{1,9},{9,1},{17,25},{25,17},{2,10},{10... | collective-permute-start | bytes 1572872 | tf_op jit(solution)/shard_map/ppermute | solution.py:72
  172.5 13.5 %collective-permute-start.5 = (bf16[1024,256]{1,0:T(8,128)(2,1)}, bf16[1024,256]{1,0:T(8,128)(2,1)}, u32[]{:S(2)}, u32[]{:S(2)}) collective-permute-start(bf16[1024,256]{1,0:T(8,128)(2,1)} %copy.76), channel_id=1, source_target_pairs={{0,16},{8,24},{16,0},{24,8},{1,17},{9,25},{17,1},{25,9},{2,18},{10... | collective-permute-start | bytes 1572872 | tf_op jit(solution)/shard_map/ppermute | solution.py:72
  187.0 6.7 %collective-permute-start.7 = (bf16[512,256]{1,0:T(8,128)(2,1)S(1)}, bf16[512,256]{1,0:T(8,128)(2,1)S(1)}, u32[]{:S(2)}, u32[]{:S(2)}) collective-permute-start(bf16[512,256]{1,0:T(8,128)(2,1)S(1)} %slice.197), channel_id=1, source_target_pairs={{0,8},{8,0},{16,24},{24,16},{1,9},{9,1},{17,25},{25,17},{2,10},{10... | collective-permute-start | bytes 786440 | tf_op jit(solution)/shard_map/ppermute | solution.py:72
  188.4 6.8 %collective-permute-start.6 = (bf16[512,256]{1,0:T(8,128)(2,1)S(1)}, bf16[512,256]{1,0:T(8,128)(2,1)S(1)}, u32[]{:S(2)}, u32[]{:S(2)}) collective-permute-start(bf16[512,256]{1,0:T(8,128)(2,1)S(1)} %slice.196), channel_id=1, source_target_pairs={{0,16},{8,24},{16,0},{24,8},{1,17},{9,25},{17,1},{25,9},{2,18},{10... | collective-permute-start | bytes 786440 | tf_op jit(solution)/shard_map/ppermute | solution.py:72
  246.9 14.4 %collective-permute-start.22 = (bf16[128,2048]{1,0:T(8,128)(2,1)S(1)}, bf16[128,2048]{1,0:T(8,128)(2,1)S(1)}, u32[]{:S(2)}, u32[]{:S(2)}) collective-permute-start(bf16[128,2048]{1,0:T(8,128)(2,1)S(1)} %get-tuple-element.42), channel_id=1, source_target_pairs={{0,16},{8,24},{16,0},{24,8},{1,17},{9,25},{17,1},{25,9},{2,18},{10... | collective-permute-start | bytes 1572872 | tf_op jit(solution)/shard_map/ppermute | solution.py:72
  248.7 12.6 %collective-permute-start.24 = (bf16[128,2048]{1,0:T(8,128)(2,1)S(1)}, bf16[128,2048]{1,0:T(8,128)(2,1)S(1)}, u32[]{:S(2)}, u32[]{:S(2)}) collective-permute-start(bf16[128,2048]{1,0:T(8,128)(2,1)S(1)} %get-tuple-element.43), channel_id=1, source_target_pairs={{0,8},{8,0},{16,24},{24,16},{1,9},{9,1},{17,25},{25,17},{2,10},{10... | collective-permute-start | bytes 1572872 | tf_op jit(solution)/shard_map/ppermute | solution.py:72
  258.2 14.9 %collective-permute-start.14 = (bf16[128,2048]{1,0:T(8,128)(2,1)S(1)}, bf16[128,2048]{1,0:T(8,128)(2,1)S(1)}, u32[]{:S(2)}, u32[]{:S(2)}) collective-permute-start(bf16[128,2048]{1,0:T(8,128)(2,1)S(1)} %get-tuple-element.44), channel_id=1, source_target_pairs={{0,16},{8,24},{16,0},{24,8},{1,17},{9,25},{17,1},{25,9},{2,18},{10... | collective-permute-start | bytes 1572872 | tf_op jit(solution)/shard_map/ppermute | solution.py:72
  260.0 14.9 %collective-permute-start.16 = (bf16[128,2048]{1,0:T(8,128)(2,1)S(1)}, bf16[128,2048]{1,0:T(8,128)(2,1)S(1)}, u32[]{:S(2)}, u32[]{:S(2)}) collective-permute-start(bf16[128,2048]{1,0:T(8,128)(2,1)S(1)} %get-tuple-element.45), channel_id=1, source_target_pairs={{0,8},{8,0},{16,24},{24,16},{1,9},{9,1},{17,25},{25,17},{2,10},{10... | collective-permute-start | bytes 1572872 | tf_op jit(solution)/shard_map/ppermute | solution.py:72
  262.7 32.9 %collective-permute-start.25 = (bf16[256,2048]{1,0:T(8,128)(2,1)}, bf16[256,2048]{1,0:T(8,128)(2,1)S(1)}, u32[]{:S(2)}, u32[]{:S(2)}) collective-permute-start(bf16[256,2048]{1,0:T(8,128)(2,1)} %pad_maximum_fusion.7), channel_id=1, source_target_pairs={{0,16},{8,24},{16,0},{24,8},{1,17},{9,25},{17,1},{25,9},{2,18},{10... | collective-permute-start | bytes 3145736 | tf_op jit(solution)/shard_map/ppermute | solution.py:72
  264.4 33.0 %collective-permute-start.23 = (bf16[256,2048]{1,0:T(8,128)(2,1)}, bf16[256,2048]{1,0:T(8,128)(2,1)}, u32[]{:S(2)}, u32[]{:S(2)}) collective-permute-start(bf16[256,2048]{1,0:T(8,128)(2,1)} %pad_maximum_fusion.6), channel_id=1, source_target_pairs={{0,8},{8,0},{16,24},{24,16},{1,9},{9,1},{17,25},{25,17},{2,10},{10... | collective-permute-start | bytes 3145736 | tf_op jit(solution)/shard_map/ppermute | solution.py:72
  276.2 38.6 %collective-permute-start.17 = (bf16[256,2048]{1,0:T(8,128)(2,1)}, bf16[256,2048]{1,0:T(8,128)(2,1)}, u32[]{:S(2)}, u32[]{:S(2)}) collective-permute-start(bf16[256,2048]{1,0:T(8,128)(2,1)} %pad_maximum_fusion.5), channel_id=1, source_target_pairs={{0,16},{8,24},{16,0},{24,8},{1,17},{9,25},{17,1},{25,9},{2,18},{10... | collective-permute-start | bytes 3145736 | tf_op jit(solution)/shard_map/ppermute | solution.py:72
  277.6 38.7 %collective-permute-start.15 = (bf16[256,2048]{1,0:T(8,128)(2,1)}, bf16[256,2048]{1,0:T(8,128)(2,1)}, u32[]{:S(2)}, u32[]{:S(2)}) collective-permute-start(bf16[256,2048]{1,0:T(8,128)(2,1)} %pad_maximum_fusion.4), channel_id=1, source_target_pairs={{0,8},{8,0},{16,24},{24,16},{1,9},{9,1},{17,25},{25,17},{2,10},{10... | collective-permute-start | bytes 3145736 | tf_op jit(solution)/shard_map/ppermute | solution.py:72
  335.5 10.0 %all-to-all-start = ((bf16[4,256,256]{2,1,0:T(8,128)(2,1)}), bf16[4,256,256]{2,1,0:T(8,128)(2,1)S(1)}, u32[]{:S(2)}, u32[]{:S(2)}) async-start(bf16[4,256,256]{2,1,0:T(8,128)(2,1)} %bitcast.263), calls=%async_computation | async-start | bytes 1048576 | tf_op jit(solution)/shard_map/all_to_all | solution.py:227
  339.0 283.0 %reduce-scatter.5.cloned.1.call-start = ((), (), s32[]{:S(2)}) async-start(), calls=%async_computation.12 | async-start | bytes 1769472 | tf_op jit(solution)/shard_map/reduce_scatter | solution.py:211
  339.6 25.0 %copy-start.26 = (f32[4,1024]{1,0:T(4,128)}, f32[4,1024]{1,0:T(4,128)S(1)}, u32[]{:S(2)}) copy-start(f32[4,1024]{1,0:T(4,128)S(1)} %log_add_fusion) | copy-start | bytes 49156
  364.6 23.8 %copy-start.37 = (bf16[1024,32]{0,1:T(8,128)(2,1)S(1)}, bf16[1024,32]{0,1:T(8,128)(2,1)}, u32[]{:S(2)}) copy-start(bf16[1024,32]{0,1:T(8,128)(2,1)} %copy-done.36) | copy-start | bytes 196612
  388.4 31.5 %copy-start.15 = (f32[1024,32]{0,1:T(8,128)S(1)}, f32[1024,32]{0,1:T(8,128)}, u32[]{:S(2)}) copy-start(f32[1024,32]{0,1:T(8,128)} %copy-done.14) | copy-start | bytes 393220
  388.4 31.5 %copy-start.17 = (f32[1024,32]{0,1:T(8,128)S(1)}, f32[1024,32]{0,1:T(8,128)}, u32[]{:S(2)}) copy-start(f32[1024,32]{0,1:T(8,128)} %copy-done.16) | copy-start | bytes 393220
  388.4 33.0 %copy-start.24 = (f32[1024,4]{0,1:T(4,128)S(1)}, f32[1024,4]{0,1:T(4,128)}, u32[]{:S(2)}) copy-start(f32[1024,4]{0,1:T(4,128)} %copy-done.23) | copy-start | bytes 49156
  427.0 203.5 %reduce-scatter.9.cloned.1.call-start = ((), (), s32[]{:S(2)}) async-start(), calls=%async_computation.14 | async-start | bytes 9437184 | tf_op jit(solution)/shard_map/reduce_scatter | solution.py:211
  450.6 36.2 %copy-start.13 = (bf16[64,4,1024]{2,0,1:T(8,128)(2,1)S(1)}, bf16[64,4,1024]{2,0,1:T(8,128)(2,1)}, u32[]{:S(2)}) copy-start(bf16[64,4,1024]{2,0,1:T(8,128)(2,1)} %copy-done.12) | copy-start | bytes 1572868
  450.7 185.2 %reduce-scatter.7.cloned.1.call-start = ((), (), s32[]{:S(2)}) async-start(), calls=%async_computation.13 | async-start | bytes 1179648 | tf_op jit(solution)/shard_map/reduce_scatter | solution.py:231
  450.7 22.3 %collective-permute-start.31 = (bf16[256,2048]{1,0:T(8,128)(2,1)}, bf16[256,2048]{1,0:T(8,128)(2,1)S(1)}, u32[]{:S(2)}, u32[]{:S(2)}) collective-permute-start(bf16[256,2048]{1,0:T(8,128)(2,1)} %get-tuple-element.22), channel_id=1, source_target_pairs={{0,16},{8,24},{16,0},{24,8},{1,17},{9,25},{17,1},{25,9},{2,18},{10... | collective-permute-start | bytes 3145736 | tf_op jit(solution)/shard_map/ppermute | solution.py:72
  452.3 24.2 %collective-permute-start.30 = (bf16[256,2048]{1,0:T(8,128)(2,1)}, bf16[256,2048]{1,0:T(8,128)(2,1)S(1)}, u32[]{:S(2)}, u32[]{:S(2)}) collective-permute-start(bf16[256,2048]{1,0:T(8,128)(2,1)} %get-tuple-element.22), channel_id=1, source_target_pairs={{0,8},{8,0},{16,24},{24,16},{1,9},{9,1},{17,25},{25,17},{2,10},{10... | collective-permute-start | bytes 3145736 | tf_op jit(solution)/shard_map/ppermute | solution.py:72
  473.0 11.0 %collective-permute-start.33 = (bf16[128,2048]{1,0:T(8,128)(2,1)S(1)}, bf16[128,2048]{1,0:T(8,128)(2,1)S(1)}, u32[]{:S(2)}, u32[]{:S(2)}) collective-permute-start(bf16[128,2048]{1,0:T(8,128)(2,1)S(1)} %slice.215), channel_id=1, source_target_pairs={{0,8},{8,0},{16,24},{24,16},{1,9},{9,1},{17,25},{25,17},{2,10},{10... | collective-permute-start | bytes 1572872 | tf_op jit(solution)/shard_map/ppermute | solution.py:72
  476.5 9.2 %collective-permute-start.32 = (bf16[128,2048]{1,0:T(8,128)(2,1)S(1)}, bf16[128,2048]{1,0:T(8,128)(2,1)S(1)}, u32[]{:S(2)}, u32[]{:S(2)}) collective-permute-start(bf16[128,2048]{1,0:T(8,128)(2,1)S(1)} %slice.214), channel_id=1, source_target_pairs={{0,16},{8,24},{16,0},{24,8},{1,17},{9,25},{17,1},{25,9},{2,18},{10... | collective-permute-start | bytes 1572872 | tf_op jit(solution)/shard_map/ppermute | solution.py:72
  491.4 149.3 %reduce-scatter.11.cloned.1.call-start = ((), (), s32[]{:S(2)}) async-start(), calls=%async_computation.15 | async-start | bytes 4718592 | tf_op jit(solution)/shard_map/reduce_scatter | solution.py:202
  502.9 30.9 %collective-permute-start.27 = (bf16[2048,384]{1,0:T(8,128)(2,1)}, bf16[2048,384]{1,0:T(8,128)(2,1)}, u32[]{:S(2)}, u32[]{:S(2)}) collective-permute-start(bf16[2048,384]{1,0:T(8,128)(2,1)} %slice.188), channel_id=1, source_target_pairs={{0,16},{8,24},{16,0},{24,8},{1,17},{9,25},{17,1},{25,9},{2,18},{10... | collective-permute-start | bytes 4718600 | tf_op jit(solution)/shard_map/ppermute | solution.py:72
  503.0 33.0 %collective-permute-start.26 = (bf16[2048,384]{1,0:T(8,128)(2,1)}, bf16[2048,384]{1,0:T(8,128)(2,1)}, u32[]{:S(2)}, u32[]{:S(2)}) collective-permute-start(bf16[2048,384]{1,0:T(8,128)(2,1)} %slice.188), channel_id=1, source_target_pairs={{0,8},{8,0},{16,24},{24,16},{1,9},{9,1},{17,25},{25,17},{2,10},{10... | collective-permute-start | bytes 4718600 | tf_op jit(solution)/shard_map/ppermute | solution.py:72
  508.6 34.8 %copy-start.22 = (bf16[1024,1,64]{0,2,1:T(8,128)(2,1)S(1)}, bf16[1024,1,64]{0,2,1:T(8,128)(2,1)}, u32[]{:S(2)}) copy-start(bf16[1024,1,64]{0,2,1:T(8,128)(2,1)} %copy-done.21) | copy-start | bytes 393220
  536.0 19.0 %collective-permute-start.29 = (bf16[1024,384]{1,0:T(8,128)(2,1)}, bf16[1024,384]{1,0:T(8,128)(2,1)}, u32[]{:S(2)}, u32[]{:S(2)}) collective-permute-start(bf16[1024,384]{1,0:T(8,128)(2,1)} %slice.210), channel_id=1, source_target_pairs={{0,8},{8,0},{16,24},{24,16},{1,9},{9,1},{17,25},{25,17},{2,10},{10... | collective-permute-start | bytes 2359304 | tf_op jit(solution)/shard_map/ppermute | solution.py:72
  538.2 18.2 %collective-permute-start.28 = (bf16[1024,384]{1,0:T(8,128)(2,1)}, bf16[1024,384]{1,0:T(8,128)(2,1)}, u32[]{:S(2)}, u32[]{:S(2)}) collective-permute-start(bf16[1024,384]{1,0:T(8,128)(2,1)} %slice.209), channel_id=1, source_target_pairs={{0,16},{8,24},{16,0},{24,8},{1,17},{9,25},{17,1},{25,9},{2,18},{10... | collective-permute-start | bytes 2359304 | tf_op jit(solution)/shard_map/ppermute | solution.py:72
  545.3 14.2 %all-to-all-start.1 = ((bf16[4,256,384]{2,1,0:T(8,128)(2,1)}), bf16[4,256,384]{2,1,0:T(8,128)(2,1)S(1)}, u32[]{:S(2)}, u32[]{:S(2)}) async-start(bf16[4,256,384]{2,1,0:T(8,128)(2,1)} %pad_maximum_fusion.8), calls=%async_computation.1 | async-start | bytes 1572864 | tf_op jit(solution)/shard_map/all_to_all | solution.py:247
  622.0 8.5 %all-to-all-start.2 = ((bf16[4,64,384]{2,1,0:T(8,128)(2,1)}), bf16[4,64,384]{2,1,0:T(8,128)(2,1)S(1)}, u32[]{:S(2)}, u32[]{:S(2)}) async-start(bf16[4,64,384]{2,1,0:T(8,128)(2,1)} %bitcast.286), calls=%async_computation.3 | async-start | bytes 393216 | tf_op jit(solution)/shard_map/all_to_all | solution.py:213
  630.5 12.9 %all-to-all-start.3 = ((bf16[4,64,2048]{2,1,0:T(8,128)(2,1)}), bf16[4,64,2048]{2,1,0:T(8,128)(2,1)S(1)}, u32[]{:S(2)}, u32[]{:S(2)}) async-start(bf16[4,64,2048]{2,1,0:T(8,128)(2,1)} %bitcast.280), calls=%async_computation.6 | async-start | bytes 2097152 | tf_op jit(solution)/shard_map/all_to_all | solution.py:213
  (37 other events, 238.0 us)
Sparse Core Ops, SparseCore 0:
  10.2 43.0 all-gather.6
  55.5 30.0 all-gather.4
  87.8 81.5 all-gather.8
  170.8 45.6 all-gather.10
  427.1 39.8 reduce-scatter.4
  469.2 87.3 reduce-scatter.8
  559.5 30.7 reduce-scatter.6
  592.5 48.1 reduce-scatter.10
